TPU v7x, 512 devices: a whole 4x8x8 slice. The times are simulated.
512 devices in a mesh: sensor: 8 (over z_lo, x), cell: 64 (over z_hi, y, core).
Axes of the slice: x: 4, y: 8, z: 8 (z_hi: 4, z_lo: 2; z = z_hi * 2 + z_lo), core: 2. Of those that a mesh axis runs over, the one named last changes fastest.
Arguments:
- swath: float32 [8, 64, 32768], P('sensor', None, 'cell'), may hold values from -6 to 6
- enc_weight: float32 [8, 64, 192], P('sensor'), may hold values from -0.4375 to 0.4375
- key_weight: float32 [64, 64], replicated, may hold values from -0.75 to 0.75
- value_weight: float32 [64, 64], replicated, may hold values from -0.75 to 0.75
- cell_query: float32 [64, 16384], P(None, 'cell'), may hold values from -6 to 6
- quality: float32 [8, 32768], P('sensor', 'cell'), may hold values from -4 to 302
- sample_cell: int32 [8, 32768], P('sensor', 'cell'), may hold values from 0 to 255
- live: int32 [8, 64], P('sensor', 'cell'), may hold values from 128 to 512
- neighbours: int32 [8, 16384], P(None, 'cell'), may hold values from 0 to 16383, as said below
- hp_weight: float32 [64, 576], replicated, may hold values from -0.25 to 0.25
Outputs:
- joined: float32 [64, 16384], P('sensor', 'cell')
Inputs may be any that keep to these rules, and one draw needn't show every extreme that they name: `neighbours`: a cell range is a patch of 16 x 16 cells, local index row * 16 + column; every neighbour lies within 257 cells of its own cell, either in the cell's own range or in an adjacent one, and then in the first column of the next range or the last column of the previous range.
All inputs are finite; a program needn't handle non-finite values.
Results may differ from a plain program's by a relative error of at most 0.0003.
Values sent between devices are 32-bit elements; how exact they have to be, the bound alone decides.
A program may use at most 64 MiB of HBM per device.

v0:
```python
import math

import jax
import jax.numpy as jnp
from jax import lax
from jax.sharding import PartitionSpec as P

floor_value = -1e30
highest = lax.Precision.HIGHEST


def passed_along(value, axis, steps):
    count = lax.axis_size(axis)
    initial, last = (max(0, -steps), min(count, count - steps))
    return lax.ppermute(value, axis, [(source, source + steps) for source in range(initial, last)])


def combined_all(value, axis, join):
    pieces = jax.tree.map(lambda part: lax.all_gather(part, axis), value)
    head = jax.tree.map(lambda part: part[0], pieces)
    tail = jax.tree.map(lambda part: part[1:], pieces)
    so_far, _ = lax.scan(lambda so_far, section: (join(so_far, section), None), head, tail)
    return so_far


def extended_2(shard, sides, width):
    for axis, dim in sides:
        devices, length = (lax.axis_size(axis), shard.shape[dim])
        up = [(i, (i + 1) % devices) for i in range(devices - 1)]
        down = [(j, i) for i, j in up]
        last = lax.slice_in_dim(shard, length - width, length, axis=dim)
        initial = lax.slice_in_dim(shard, 0, width, axis=dim)
        before = lax.ppermute(last, axis, up)
        after = lax.ppermute(initial, axis, down)
        shard = jnp.concatenate([before, shard, after], axis=dim)
    return shard


def combine_pools(first, second):
    first_peak, first_total, first_sum = first
    second_peak, second_total, second_sum = second
    joint = jnp.maximum(first_peak, second_peak)
    first_factor = jnp.exp(first_peak - joint)
    second_factor = jnp.exp(second_peak - joint)
    return (
        joint,
        first_total * first_factor + second_total * second_factor,
        first_sum * first_factor[None, :] + second_sum * second_factor[None, :],
    )


def stencil(cube, centre, gathered):
    return jnp.dot(cube[:, 0, :], centre, precision=highest) + jnp.einsum(
        "oki,ikc->oc", cube[:, 1:, :], gathered, precision=highest
    )


def on_device(
    swath,
    enc_weight,
    key_weight,
    value_weight,
    cell_query,
    quality,
    sample_cell,
    live,
    neighbours,
    hp_weight,
):
    signal = swath[0]
    channels = signal.shape[0]
    sample_count = signal.shape[1]
    cell_count = cell_query.shape[1]
    tail_cols = passed_along(signal[:, sample_count - 2 :], "cell", 1)
    padded = jnp.concatenate([tail_cols, signal], axis=1)
    stacked = jnp.concatenate(
        [
            padded[:, 0:sample_count],
            padded[:, 1 : sample_count + 1],
            padded[:, 2 : sample_count + 2],
        ],
        axis=0,
    )
    encoded = jax.nn.gelu(jnp.dot(enc_weight[0], stacked, precision=highest), approximate=False)
    key_rows = jnp.dot(key_weight, encoded, precision=highest)
    value_rows = jnp.dot(value_weight, encoded, precision=highest)
    range_start = lax.axis_index("cell") * cell_count
    local_cell = sample_cell[0]
    query_rows = jnp.take(cell_query, local_cell, axis=1)
    inv_root = 1.0 / math.sqrt(channels)
    score = jnp.sum(query_rows * key_rows, axis=0) * inv_root + quality[0]
    valid = jnp.arange(sample_count, dtype=jnp.int32) < live[0, 0]
    local_peak = jnp.maximum(
        jax.ops.segment_max(jnp.where(valid, score, -jnp.inf), local_cell, cell_count), floor_value
    )
    weights_exp = jnp.where(valid, jnp.exp(score - local_peak[local_cell]), 0.0)
    local_total = jax.ops.segment_sum(weights_exp, local_cell, cell_count)
    local_sum = jax.ops.segment_sum((value_rows * weights_exp[None, :]).T, local_cell, cell_count).T
    prior_key = jnp.dot(key_weight, cell_query, precision=highest)
    prior_score = jnp.sum(cell_query * prior_key, axis=0) * inv_root
    hp_cube = hp_weight.reshape(hp_weight.shape[0], -1, channels)
    out_rows = channels // lax.axis_size("sensor")
    peak_all, total_all, sum_all = combined_all(
        (local_peak, local_total, local_sum), "sensor", combine_pools
    )
    prior_value = jnp.dot(value_weight, cell_query, precision=highest)
    joint = jnp.maximum(peak_all, prior_score)
    pool_factor = jnp.exp(peak_all - joint)
    prior_factor = jnp.exp(prior_score - joint)
    pooled = (sum_all * pool_factor[None, :] + prior_value * prior_factor[None, :]) / (
        total_all * pool_factor + prior_factor
    )[None, :]
    extended = extended_2(pooled, (("cell", 1),), cell_count)
    gathered = jnp.take(extended, neighbours - range_start + cell_count, axis=1)
    own_cube = lax.dynamic_slice_in_dim(hp_cube, lax.axis_index("sensor") * out_rows, out_rows, 0)
    joined = stencil(own_cube, pooled, gathered)
    return joined


def solution(mesh):
    in_specs = (
        P("sensor", None, "cell"),
        P("sensor", None, None),
        P(),
        P(),
        P(None, "cell"),
        P("sensor", "cell"),
        P("sensor", "cell"),
        P("sensor", "cell"),
        P(None, "cell"),
        P(),
    )
    out_specs = P("sensor", "cell")
    return jax.shard_map(
        on_device, mesh=mesh, in_specs=in_specs, out_specs=out_specs, check_vma=False
    )
```

profile of v0, /device:TPU:187, one launch (start us, length us, event | category | flops | bytes accessed | tf_op | source)
XLA Modules:
  0.0 118.3 jit_solution(13270562354278115097)
XLA Ops:
  0.0 0.0 copy-start
  0.0 0.0 copy-start.2
  0.0 0.0 copy-start.9
  0.0 0.9 slice.60
  0.9 6.8 %collective-permute-start = (f32[64,2]{1,0:T(8,128)S(1)}, f32[64,2]{1,0:T(8,128)S(1)}, u32[]{:S(2)}, u32[]{:S(2)}) collective-permute-start(f32[64,2]{1,0:T(8,128)S(1)} %slice.60), channel_id=1, source_target_pairs={{0,1},{1,2},{2,3},{3,4},{4,5},{5,6},{6,7},{7,8},{8,9},{9,10},{10,1... | collective-permute-start | bytes 1544 | tf_op jit(solution)/shard_map/ppermute | solution.py:15
  7.7 0.0 copy-done.9
  7.7 0.0 copy-start.11
  7.7 0.7 copy-done.11
  8.4 0.0 copy-done.2
  8.4 0.1 copy.35
  8.5 1.0 gather_fusion
  9.6 0.0 copy-start.5
  9.6 0.0 copy-start.4
  9.6 0.1 copy.36
  10.4 0.0 copy-done.5
  10.4 0.2 fusion.4
  10.6 0.0 copy-done.4
  10.6 0.0 copy-start.3
  10.6 0.1 copy.33
  10.8 0.0 collective-permute-done
  10.8 0.7 copy-done.3
  11.5 0.1 fusion.18
  11.6 0.0 copy-done
  11.6 0.7 fusion.20
  12.3 0.3 fusion.1
  12.6 0.0 copy-start.10
  12.6 0.7 copy-done.10
  13.3 4.1 %scatter_custom_fusion = f32[256]{0:T(256)S(1)} fusion(s32[512]{0:T(512)S(1)} %bitcast.150, f32[512]{0:T(512)S(1)} %fusion.43, f32[]{:T(128)} %constant.20.clone.1), kind=kCustom, calls=%fused_computation.90 | custom fusion | flops 512 | bytes 1028 | tf_op jit(solution)/shard_map/scatter-max | solution.py:94
  17.4 0.0 copy-start.8
  17.4 3.5 %gather_fusion.1 = f32[512]{0:T(512)S(1)} fusion(f32[256]{0:T(256)S(1)} %broadcast_maximum_fusion, s32[1024]{0:T(1024)S(1)} %pad_clamp_fusion), kind=kCustom, calls=%fused_computation.1 | custom fusion | bytes 6144 | tf_op jit(solution)/shard_map/gather | solution.py:96
  21.0 0.0 copy-done.8
  21.0 0.3 convolution_multiply_fusion
  21.3 0.1 copy.37
  21.4 2.3 %scatter_custom_fusion.2 = f32[256,64]{1,0:T(8,128)S(1)} fusion(s32[512]{0:T(512)S(1)} %bitcast.151, f32[512,64]{1,0:T(8,128)S(1)} %copy.37, f32[]{:T(128)} %constant.69.clone.1), kind=kCustom, calls=%fused_computation.63 | custom fusion | flops 32768 | bytes 65540 | tf_op jit(solution)/shard_map/scatter-add | solution.py:98
  23.7 0.1 copy.38
  23.8 23.4 %all-gather.2 = f32[512,256]{1,0:T(8,128)S(1)} all-gather(f32[64,256]{1,0:T(8,128)S(1)} %copy.38), channel_id=4, replica_groups=mesh['sensor'=8,'cell'=64] {'sensor'}, dimensions={0}, use_global_device_ids=true | all-gather | bytes 589824 | tf_op jit(solution)/shard_map/all_gather | solution.py:19
  47.2 0.0 copy-start.1
  47.2 0.8 copy-done.1
  48.0 0.0 slice-start
  48.0 4.1 %scatter_custom_fusion.1 = f32[256]{0:T(256)S(1)} fusion(s32[512]{0:T(512)S(1)} %bitcast.152, f32[512]{0:T(512)S(1)} %get-tuple-element.85, f32[]{:T(128)} %constant.69.clone.1), kind=kCustom, calls=%fused_computation.87 | custom fusion | flops 512 | bytes 1028 | tf_op jit(solution)/shard_map/scatter-add | solution.py:97
  52.1 12.2 %all-gather.4 = f32[8,1,256]{2,1,0:T(1,128)S(1)} all-gather(f32[1,1,256]{2,1,0:T(1,128)S(1)} %bitcast.154), channel_id=3, replica_groups=mesh['sensor'=8,'cell'=64] {'sensor'}, dimensions={0}, use_global_device_ids=true | all-gather | bytes 9216 | tf_op jit(solution)/shard_map/all_gather | solution.py:19
  64.2 0.0 copy-start.6
  64.2 0.6 copy-done.6
  64.8 14.7 %all-gather.3 = f32[8,1,256]{2,1,0:T(1,128)S(1)} all-gather(f32[1,1,256]{2,1,0:T(1,128)S(1)} %bitcast.128), channel_id=2, replica_groups=mesh['sensor'=8,'cell'=64] {'sensor'}, dimensions={0}, use_global_device_ids=true | all-gather | bytes 9216 | tf_op jit(solution)/shard_map/all_gather | solution.py:19
  79.5 0.0 copy-start.7
  79.5 0.6 copy-done.7
  80.1 0.0 slice-start.2
  80.1 0.0 slice-start.1
  80.1 0.0 slice-done
  80.2 0.7 slice-done.2
  80.8 0.0 slice-done.1
  80.8 0.5 while.14
  81.4 0.2 fusion.3
  81.6 19.0 %collective-permute-start.1 = (f32[64,256]{1,0:T(8,128)S(1)}, f32[64,256]{1,0:T(8,128)S(1)}, u32[]{:S(2)}, u32[]{:S(2)}) collective-permute-start(f32[64,256]{1,0:T(8,128)S(1)} %fusion.3), channel_id=1, source_target_pairs={{0,1},{1,2},{2,3},{3,4},{4,5},{5,6},{6,7},{7,8},{8,9},{9,10},{10,1... | collective-permute-start | bytes 196616 | tf_op jit(solution)/shard_map/ppermute | solution.py:33
  100.6 1.9 %collective-permute-start.2 = (f32[64,256]{1,0:T(8,128)S(1)}, f32[64,256]{1,0:T(8,128)S(1)}, u32[]{:S(2)}, u32[]{:S(2)}) collective-permute-start(f32[64,256]{1,0:T(8,128)S(1)} %fusion.3), channel_id=1, source_target_pairs={{1,0},{2,1},{3,2},{4,3},{5,4},{6,5},{7,6},{8,7},{9,8},{10,9},{11,1... | collective-permute-start | bytes 196616 | tf_op jit(solution)/shard_map/ppermute | solution.py:34
  102.5 0.3 fusion.41
  102.8 0.0 collective-permute-done.1
  102.8 8.2 %collective-permute-done.2 = f32[64,256]{1,0:T(8,128)S(1)} collective-permute-done((f32[64,256]{1,0:T(8,128)S(1)}, f32[64,256]{1,0:T(8,128)S(1)}, u32[]{:S(2)}, u32[]{:S(2)}) %collective-permute-start.2) | collective-permute-done | bytes 65568 | tf_op jit(solution)/shard_map/ppermute | solution.py:34
  111.1 0.2 copy.39
  111.2 5.5 %gather_fusion.2 = f32[2048,64]{1,0:T(8,128)S(1)} fusion(f32[64,768]{0,1:T(8,128)S(1)} %copy.39, s32[2048]{0:T(1024)S(1)} %broadcast_clamp_fusion), kind=kCustom, calls=%fused_computation.2 | custom fusion | bytes 1056768 | tf_op jit(solution)/shard_map/jit(_take)/gather | solution.py:114
  116.7 0.3 copy.40
  117.0 1.3 %fusion.5 = f32[8,256]{1,0:T(8,128)} fusion(f32[8,256]{1,0:T(8,128)S(1)} %fusion.41, f32[8,256,64]{1,2,0:T(8,128)S(1)} %copy.40, f32[64,9,64]{0,2,1:T(8,128)S(1)} %bitcast.132, s32[]{:T(128)S(6)} %select_n.43, pred[8,256]{1,0:T(8,128)(4,1)S(1)} %compare_and_fusion), kind=kOutput, calls=%fused_computation.22 | convolution fusion | flops 12716032 | bytes 690180 | tf_op jit(solution)/shard_map/oki,ikc->oc/dot_general | solution.py:53
  (39 shorter events, 0.5 us)
Async XLA Ops:
  0.0 11.6 %copy-start = (f32[1,64,192]{2,1,0:T(8,128)S(1)}, f32[1,64,192]{2,1,0:T(8,128)}, u32[]{:S(2)}) copy-start(f32[1,64,192]{2,1,0:T(8,128)} %param.13) | copy-start | bytes 147460
  0.0 8.4 %copy-start.2 = (f32[64,256]{1,0:T(8,128)S(1)}, f32[64,256]{1,0:T(8,128)}, u32[]{:S(2)}) copy-start(f32[64,256]{1,0:T(8,128)} %param.16) | copy-start | bytes 196612
  0.0 7.7 %copy-start.9 = (s32[8,256]{1,0:T(8,128)S(1)}, s32[8,256]{1,0:T(8,128)}, u32[]{:S(2)}) copy-start(s32[8,256]{1,0:T(8,128)} %param.20) | copy-start | bytes 24580
  0.9 9.9 %collective-permute-start = (f32[64,2]{1,0:T(8,128)S(1)}, f32[64,2]{1,0:T(8,128)S(1)}, u32[]{:S(2)}, u32[]{:S(2)}) collective-permute-start(f32[64,2]{1,0:T(8,128)S(1)} %slice.60), channel_id=1, source_target_pairs={{0,1},{1,2},{2,3},{3,4},{4,5},{5,6},{6,7},{7,8},{8,9},{9,10},{10,1... | collective-permute-start | bytes 1544 | tf_op jit(solution)/shard_map/ppermute | solution.py:15
  7.7 0.7 copy-start.11
  9.6 0.8 copy-start.5
  9.6 1.0 copy-start.4
  10.6 0.9 copy-start.3
  12.6 0.7 copy-start.10
  17.4 3.6 %copy-start.8 = (f32[64,64]{1,0:T(8,128)S(1)}, f32[64,64]{1,0:T(8,128)}, u32[]{:S(2)}) copy-start(f32[64,64]{1,0:T(8,128)} %param.15) | copy-start | bytes 49156
  47.2 0.8 copy-start.1
  48.0 32.2 %slice-start = ((f32[512,256]{1,0:T(8,128)}), f32[64,256]{1,0:T(8,128)S(1)}, s32[]{:S(2)}) async-start(f32[512,256]{1,0:T(8,128)} %copy-done.1), calls=%async_computation | async-start | bytes 131072 | tf_op jit(solution)/shard_map/slice | solution.py:20
  64.2 0.6 copy-start.6
  79.5 0.6 copy-start.7
  80.1 0.7 slice-start.2
  80.1 0.7 slice-start.1
  81.6 21.2 %collective-permute-start.1 = (f32[64,256]{1,0:T(8,128)S(1)}, f32[64,256]{1,0:T(8,128)S(1)}, u32[]{:S(2)}, u32[]{:S(2)}) collective-permute-start(f32[64,256]{1,0:T(8,128)S(1)} %fusion.3), channel_id=1, source_target_pairs={{0,1},{1,2},{2,3},{3,4},{4,5},{5,6},{6,7},{7,8},{8,9},{9,10},{10,1... | collective-permute-start | bytes 196616 | tf_op jit(solution)/shard_map/ppermute | solution.py:33
  100.6 10.4 %collective-permute-start.2 = (f32[64,256]{1,0:T(8,128)S(1)}, f32[64,256]{1,0:T(8,128)S(1)}, u32[]{:S(2)}, u32[]{:S(2)}) collective-permute-start(f32[64,256]{1,0:T(8,128)S(1)} %fusion.3), channel_id=1, source_target_pairs={{1,0},{2,1},{3,2},{4,3},{5,4},{6,5},{7,6},{8,7},{9,8},{10,9},{11,1... | collective-permute-start | bytes 196616 | tf_op jit(solution)/shard_map/ppermute | solution.py:34
where the time goes:
time: 119 us; the launch traced here: 118 us
  blocking collectives  50.3 us (42%)
  starting transfers between devices  27.7 us (23%)
  local copies, waits for them, and re-layouts  16.7 us (14%)
  other arithmetic  10.9 us (9%)
  waiting for transfers between devices  8.24 us (7%)
  matrix products  3.19 us (3%)
    all_gather x3, blocking collectives, combined_all(): pieces = jax.tree.map(lambda part: lax.all_gather(part, axis), value)  50.3 us
    ppermute x1, starting transfers between devices, extended_2(): before = lax.ppermute(last, axis, up)  19 us
    ppermute x1, waiting for transfers between devices, extended_2(): after = lax.ppermute(initial, axis, down)  8.23 us
    ppermute x1, starting transfers between devices, passed_along(): lax.ppermute(value, axis, [(source, source + steps) for source in range(i...  6.78 us
    gather x2, local copies, waits for them, and re-layouts, on_device(): gathered = jnp.take(extended, neighbours - range_start + cell_count, axis=1)  5.77 us
    unnamed x29, local copies, waits for them, and re-layouts  4.29 us
    scatter-add x1, other arithmetic, on_device(): local_total = jax.ops.segment_sum(weights_exp, local_cell, cell_count)  4.08 us
    another operation x1, other arithmetic, on_device(): jax.ops.segment_max(jnp.where(valid, score, -jnp.inf), local_cell, cell_c...  4.08 us
  transfers between devices with their start and end apart: 3, of which 1 were waited for; matrix products, arithmetic and copies ran while one was open for 2% of the time, Pallas kernels for 0%

commit v1 on v0

v1 whole, which is shorter than its diff:
```python
import jax
import jax.numpy as jnp
from jax import lax
from jax.experimental import pallas as pl
from jax.experimental.pallas import tpu as pltpu
from jax.sharding import PartitionSpec as P

MESH = pl.DeviceIdType.MESH
FLOOR = -1e30
HIGHEST = lax.Precision.HIGHEST
OFFSETS = ((1, 2), (0, 2), (1, 1), (1, 3), (0, 1), (0, 3), (1, 0))


def dot(a, b, dims=((1,), (0,)), precision=HIGHEST):
    return lax.dot_general(
        a, b, (dims, ((), ())), precision=precision, preferred_element_type=jnp.float32
    )


def lanes(values, index):
    return jnp.take_along_axis(values, index, axis=1, mode="promise_in_bounds")


def split3(x):
    high = x.astype(jnp.bfloat16)
    rest = x - high.astype(jnp.float32)
    mid = rest.astype(jnp.bfloat16)
    low = (rest - mid.astype(jnp.float32)).astype(jnp.bfloat16)
    return jnp.concatenate([high, mid, low], axis=0)


def gelu(x):
    return 0.5 * x * (1.0 + lax.erf(x * 0.7071067811865476))


def kernel(
    swath_ref,
    enc_ref,
    key_ref,
    value_ref,
    query_ref,
    quality_ref,
    cell_ref,
    live_ref,
    near_ref,
    hp_ref,
    out_ref,
    x_s,
    enc_s,
    key_s,
    value_s,
    query_s,
    quality_s,
    cell_s,
    live_s,
    near_s,
    hp_s,
    tail_s,
    send_s,
    part_s,
    pool_s,
    prev_s,
    next_s,
    in_sem,
    tail_sem,
    part_out,
    part_in,
    pool_out,
    pool_in,
    up_out,
    up_in,
    down_out,
    down_in,
):
    s = lax.axis_index("sensor")
    c = lax.axis_index("cell")
    z, x = s // 4, s % 4
    up, down = (c + 1) % 64, (c + 63) % 64

    def partner(dz, dx):
        return ((z + dz) % 2) * 4 + (x + dx) % 4

    loads = [
        pltpu.make_async_copy(source, target, in_sem.at[i])
        for i, (source, target) in enumerate(
            (
                (cell_ref, cell_s),
                (query_ref, query_s),
                (key_ref, key_s),
                (enc_ref.at[0], enc_s),
                (swath_ref.at[0], x_s),
                (quality_ref, quality_s),
                (live_ref, live_s),
                (hp_ref.at[pl.ds(pl.multiple_of(s * 8, 8), 8)], hp_s),
                (value_ref, value_s),
                (near_ref, near_s),
            )
        )
    ]
    for load in loads:
        load.start()

    barrier = pltpu.get_barrier_semaphore()
    for target in (up, down):
        pl.semaphore_signal(barrier, inc=1, device_id=(s, target), device_id_type=MESH)
    for dz, dx in OFFSETS:
        pl.semaphore_signal(
            barrier, inc=1, device_id=(partner(dz, dx), c), device_id_type=MESH
        )
    pl.semaphore_wait(barrier, 9)

    tail = pltpu.make_async_remote_copy(
        src_ref=swath_ref.at[0, :, pl.ds(384, 128)],
        dst_ref=tail_s,
        send_sem=tail_sem.at[0],
        recv_sem=tail_sem.at[1],
        device_id=(s, up),
        device_id_type=MESH,
    )
    tail.start()

    for i in range(3):
        loads[i].wait()
    query = query_s[...]
    bilinear = dot(key_s[...], query, ((0,), (0,))) * 0.125
    prior = jnp.sum(query * bilinear, axis=0, keepdims=True)
    cell = cell_s[...]
    asked = []
    for b in range(4):
        index = jnp.broadcast_to(cell[:, b * 128 : (b + 1) * 128], (64, 128))
        asked.append(
            jnp.where(
                index >= 128,
                lanes(bilinear[:, 128:], index & 127),
                lanes(bilinear[:, :128], index & 127),
            )
        )
    hot = lax.broadcasted_iota(jnp.int32, (256, 512), 0) == cell

    for i in range(3, 7):
        loads[i].wait()
    enc = enc_s[...]
    taps = jnp.concatenate([enc[:, 0:64], enc[:, 64:128], enc[:, 128:192]], axis=0)
    mixed = dot(taps, x_s[...])
    two, one, zero = mixed[0:64], mixed[64:128], mixed[128:192]
    rest = zero + pltpu.roll(one, 1, 1) + pltpu.roll(two, 2, 1)
    quality = quality_s[...]
    valid = lax.broadcasted_iota(jnp.int32, (1, 512), 1) < live_s[0, 0]

    def scored(encoded, b):
        return (
            jnp.sum(encoded * asked[b], axis=0, keepdims=True)
            + quality[:, b * 128 : (b + 1) * 128]
        )

    encoded = [None] + [gelu(rest[:, b * 128 : (b + 1) * 128]) for b in range(1, 4)]
    score = [None] + [scored(encoded[b], b) for b in range(1, 4)]

    for i in range(7, 10):
        loads[i].wait()
    hp = hp_s[...]
    stacked = jnp.concatenate([hp[:, k * 64 : (k + 1) * 64] for k in range(9)], axis=0)
    stencil = dot(stacked, value_s[...])
    near = near_s[...] - c * 256
    near_edge = ((near >> 4) & 15) + jnp.where(near < 0, 16, 0)
    near_side = (near < 0) | (near >= 256)

    tail.wait_recv()
    lane = lax.broadcasted_iota(jnp.int32, (64, 128), 1)
    before = dot(taps[0:128], jnp.where(c > 0, tail_s[...], 0.0))
    first = (
        zero[:, :128]
        + pltpu.roll(jnp.where(lane == 127, before[64:128], one[:, :128]), 1, 1)
        + pltpu.roll(jnp.where(lane >= 126, before[0:64], two[:, :128]), 2, 1)
    )
    encoded[0] = gelu(first)
    score[0] = scored(encoded[0], 0)

    encoded = jnp.concatenate(encoded, axis=1)
    score = jnp.concatenate(score, axis=1)
    peak = jnp.max(
        jnp.where(hot, jnp.where(valid, score, FLOOR), FLOOR), axis=1, keepdims=True
    )
    own_peak = jnp.max(jnp.where(hot, peak, FLOOR), axis=0, keepdims=True)
    weight = jnp.where(valid, jnp.exp(score - own_peak), 0.0)
    weighted = jnp.concatenate(
        [encoded * weight, jnp.broadcast_to(weight, (8, 512))], axis=0
    )
    sums = dot(
        split3(weighted),
        jnp.where(hot, 1.0, 0.0).astype(jnp.bfloat16),
        ((1,), (1,)),
        None,
    )
    sums = sums[0:72] + (sums[72:144] + sums[144:216])
    eye = lax.broadcasted_iota(jnp.int32, (256, 256), 0) == lax.broadcasted_iota(
        jnp.int32, (256, 256), 1
    )
    peak_row = jnp.max(jnp.where(eye, peak, FLOOR), axis=0, keepdims=True)
    extra = jnp.concatenate([peak_row, sums[64:65]], axis=0)
    for k in range(8):
        send_s[k, 0:8] = sums[k * 8 : (k + 1) * 8]
        send_s[k, 8:10] = extra

    parts = []
    for dz, dx in OFFSETS:
        slot = dz * 4 + dx
        copy = pltpu.make_async_remote_copy(
            src_ref=send_s.at[partner(dz, dx)],
            dst_ref=part_s.at[slot],
            send_sem=part_out.at[slot],
            recv_sem=part_in.at[slot],
            device_id=(partner(dz, dx), c),
            device_id_type=MESH,
        )
        copy.start()
        parts.append(copy)
    own = send_s[s]
    for copy in parts:
        copy.wait_recv()
    blocks = [own] + [part_s[k] for k in range(1, 8)]
    peaks = jnp.concatenate([block[8:9] for block in blocks], axis=0)
    totals = jnp.concatenate([block[9:10] for block in blocks], axis=0)
    joint = jnp.maximum(jnp.max(peaks, axis=0, keepdims=True), prior)
    factor = jnp.exp(peaks - joint)
    prior_factor = jnp.exp(prior - joint)
    below = jnp.sum(totals * factor, axis=0, keepdims=True) + prior_factor
    above = query_s[pl.ds(pl.multiple_of(s * 8, 8), 8), :] * prior_factor
    for k in range(8):
        above = above + blocks[k][0:8] * factor[k : k + 1]
    pooled = above / below
    edge = lax.broadcasted_iota(jnp.int32, (8, 128), 1)
    edge_cell = (edge & 15) * 16 + jnp.where((edge & 16) > 0, 15, 0)
    pool_s[s, :, 0:256] = pooled
    pool_s[s, :, 256:384] = jnp.where(
        edge_cell >= 128,
        lanes(pooled[:, 128:], edge_cell & 127),
        lanes(pooled[:, :128], edge_cell & 127),
    )

    ups, downs, pools = [], [], []
    for dz, dx in OFFSETS + ((0, 0),):
        slot = dz * 4 + dx
        to = partner(dz, dx)
        for cell_to, target, out, into, kept in (
            (up, prev_s, up_out, up_in, ups),
            (down, next_s, down_out, down_in, downs),
        ):
            copy = pltpu.make_async_remote_copy(
                src_ref=pool_s.at[s, :, pl.ds(256, 128)],
                dst_ref=target.at[s],
                send_sem=out.at[slot],
                recv_sem=into.at[slot],
                device_id=(to, cell_to),
                device_id_type=MESH,
            )
            copy.start()
            kept.append(copy)
        if slot:
            copy = pltpu.make_async_remote_copy(
                src_ref=pool_s.at[s, :, pl.ds(0, 256)],
                dst_ref=pool_s.at[s, :, pl.ds(0, 256)],
                send_sem=pool_out.at[slot],
                recv_sem=pool_in.at[slot],
                device_id=(to, c),
                device_id_type=MESH,
            )
            copy.start()
            pools.append(copy)
    for copy in pools:
        copy.wait_recv()
    inner = dot(stencil, pool_s[:, :, 0:256].reshape(64, 256))
    joined = inner[0:8]
    picked = []
    for k in range(8):
        index = jnp.broadcast_to(near[k : k + 1], (8, 256))
        row = inner[8 + k * 8 : 16 + k * 8]
        halves = []
        for h in range(2):
            part = index[:, h * 128 : (h + 1) * 128]
            halves.append(
                jnp.where(
                    (part & 128) > 0,
                    lanes(row[:, 128:], part & 127),
                    lanes(row[:, :128], part & 127),
                )
            )
        picked.append(halves)
    for copy in ups + downs:
        copy.wait_recv()
    sides = jnp.where(
        lane < 16, next_s[...].reshape(64, 128), prev_s[...].reshape(64, 128)
    )
    outer = dot(stencil[8:72], sides)
    for h in range(2):
        total = joined[:, h * 128 : (h + 1) * 128]
        for k in range(8):
            cut = slice(h * 128, (h + 1) * 128)
            index = jnp.broadcast_to(near_edge[k : k + 1, cut], (8, 128))
            side = jnp.broadcast_to(near_side[k : k + 1, cut], (8, 128))
            total = total + jnp.where(
                side, lanes(outer[k * 8 : (k + 1) * 8], index), picked[k][h]
            )
        out_ref[:, h * 128 : (h + 1) * 128] = total

    tail.wait_send()
    for copy in parts + pools + ups + downs:
        copy.wait_send()


def on_device(*operands):
    f32, i32 = jnp.float32, jnp.int32
    dma = pltpu.SemaphoreType.DMA
    return pl.pallas_call(
        kernel,
        out_shape=jax.ShapeDtypeStruct((8, 256), f32),
        in_specs=[pl.BlockSpec(memory_space=pltpu.HBM)] * 10,
        out_specs=pl.BlockSpec(memory_space=pltpu.VMEM),
        scratch_shapes=[
            pltpu.VMEM((64, 512), f32),
            pltpu.VMEM((64, 192), f32),
            pltpu.VMEM((64, 64), f32),
            pltpu.VMEM((64, 64), f32),
            pltpu.VMEM((64, 256), f32),
            pltpu.VMEM((1, 512), f32),
            pltpu.VMEM((1, 512), i32),
            pltpu.SMEM((1, 1), i32),
            pltpu.VMEM((8, 256), i32),
            pltpu.VMEM((8, 576), f32),
            pltpu.VMEM((64, 128), f32),
            pltpu.VMEM((8, 10, 256), f32),
            pltpu.VMEM((8, 10, 256), f32),
            pltpu.VMEM((8, 8, 384), f32),
            pltpu.VMEM((8, 8, 128), f32),
            pltpu.VMEM((8, 8, 128), f32),
            dma((10,)),
            dma((2,)),
        ]
        + [dma((8,))] * 8,
        compiler_params=pltpu.CompilerParams(collective_id=0, has_side_effects=True),
    )(*operands)


def solution(mesh):
    in_specs = (
        P("sensor", None, "cell"),
        P("sensor", None, None),
        P(),
        P(),
        P(None, "cell"),
        P("sensor", "cell"),
        P("sensor", "cell"),
        P("sensor", "cell"),
        P(None, "cell"),
        P(),
    )
    return jax.shard_map(
        on_device,
        mesh=mesh,
        in_specs=in_specs,
        out_specs=P("sensor", "cell"),
        check_vma=False,
    )
```

time: 119 us -> 31.4 us (0.26)
  the two profiles are of different devices: /device:TPU:187 before, /device:TPU:1 now
where the time goes in v1:
time: 31.4 us; the launch traced here: 31.2 us
  Pallas kernels  29.3 us (93%)
  local copies, waits for them, and re-layouts  1.3 us (4%)
  between operations  0.66 us (2%)
    pallas_call x1, Pallas kernels, on_device(): pl.pallas_call(kernel, out_shape=jax.ShapeDtypeStruct((8, 256), f32), in_...  29.3 us
    unnamed x1, local copies, waits for them, and re-layouts  1.3 us

profile of v1, /device:TPU:1, one launch (start us, length us, event | category | flops | bytes accessed | tf_op | source)
XLA Modules:
  0.0 31.2 jit_solution(10089945632904820474)
XLA Ops:
  0.7 29.3 %shard_map.100 = f32[8,256]{1,0:T(8,128)} custom-call(f32[1,64,512]{2,1,0:T(8,128)} %swath_ref.1, f32[1,64,192]{2,1,0:T(8,128)} %enc_ref.1, f32[64,64]{1,0:T(8,128)} %key_ref.1, f32[64,64]{1,0:T(8,128)} %value_ref.1, f32[64,256]{1,0:T(8,128)} %query_ref.1, f32[1,512]{1,0:T(1,128)} %quality_ref.1, s32[1,512]{1,0:T(1,128)} %cell_ref.1, ...), custom_call_target="tpu_custom_call" | custom-call | tf_op jit(solution)/shard_map/pallas_call | solution.py:314
  29.9 1.3 %copy.13 = f32[8,256]{1,0:T(8,128)} copy(f32[8,256]{1,0:T(8,128)} %shard_map.100) | data formatting | bytes 16384

commit v2 on v1

--- a/solution.py
+++ b/solution.py
@@ -52,7 +52,6 @@
     query_s,
     quality_s,
     cell_s,
-    live_s,
     near_s,
     hp_s,
     tail_s,
@@ -75,7 +74,8 @@
     s = lax.axis_index("sensor")
     c = lax.axis_index("cell")
     z, x = s // 4, s % 4
-    up, down = (c + 1) % 64, (c + 63) % 64
+    up, down = c + 1, c - 1
+    has_up, has_down = c < 63, c > 0
 
     def partner(dz, dx):
         return ((z + dz) % 2) * 4 + (x + dx) % 4
@@ -90,7 +90,6 @@
                 (enc_ref.at[0], enc_s),
                 (swath_ref.at[0], x_s),
                 (quality_ref, quality_s),
-                (live_ref, live_s),
                 (hp_ref.at[pl.ds(pl.multiple_of(s * 8, 8), 8)], hp_s),
                 (value_ref, value_s),
                 (near_ref, near_s),
@@ -101,13 +100,21 @@
         load.start()
 
     barrier = pltpu.get_barrier_semaphore()
-    for target in (up, down):
-        pl.semaphore_signal(barrier, inc=1, device_id=(s, target), device_id_type=MESH)
+    for target, there in ((up, has_up), (down, has_down)):
+
+        @pl.when(there)
+        def _():
+            pl.semaphore_signal(
+                barrier, inc=1, device_id=(s, target), device_id_type=MESH
+            )
+
     for dz, dx in OFFSETS:
         pl.semaphore_signal(
             barrier, inc=1, device_id=(partner(dz, dx), c), device_id_type=MESH
         )
-    pl.semaphore_wait(barrier, 9)
+    pl.semaphore_wait(
+        barrier, 7 + has_up.astype(jnp.int32) + has_down.astype(jnp.int32)
+    )
 
     tail = pltpu.make_async_remote_copy(
         src_ref=swath_ref.at[0, :, pl.ds(384, 128)],
@@ -117,7 +124,19 @@
         device_id=(s, up),
         device_id_type=MESH,
     )
-    tail.start()
+
+    @pl.when(has_up)
+    def _():
+        tail.start()
+
+    @pl.when(jnp.logical_not(has_down))
+    def _():
+        tail_s[...] = jnp.zeros((64, 128), jnp.float32)
+        prev_s[...] = jnp.zeros((8, 8, 128), jnp.float32)
+
+    @pl.when(jnp.logical_not(has_up))
+    def _():
+        next_s[...] = jnp.zeros((8, 8, 128), jnp.float32)
 
     for i in range(3):
         loads[i].wait()
@@ -137,7 +156,7 @@
         )
     hot = lax.broadcasted_iota(jnp.int32, (256, 512), 0) == cell
 
-    for i in range(3, 7):
+    for i in range(3, 6):
         loads[i].wait()
     enc = enc_s[...]
     taps = jnp.concatenate([enc[:, 0:64], enc[:, 64:128], enc[:, 128:192]], axis=0)
@@ -145,7 +164,7 @@
     two, one, zero = mixed[0:64], mixed[64:128], mixed[128:192]
     rest = zero + pltpu.roll(one, 1, 1) + pltpu.roll(two, 2, 1)
     quality = quality_s[...]
-    valid = lax.broadcasted_iota(jnp.int32, (1, 512), 1) < live_s[0, 0]
+    valid = lax.broadcasted_iota(jnp.int32, (1, 512), 1) < live_ref[0, 0]
 
     def scored(encoded, b):
         return (
@@ -156,7 +175,7 @@
     encoded = [None] + [gelu(rest[:, b * 128 : (b + 1) * 128]) for b in range(1, 4)]
     score = [None] + [scored(encoded[b], b) for b in range(1, 4)]
 
-    for i in range(7, 10):
+    for i in range(6, 9):
         loads[i].wait()
     hp = hp_s[...]
     stacked = jnp.concatenate([hp[:, k * 64 : (k + 1) * 64] for k in range(9)], axis=0)
@@ -165,9 +184,12 @@
     near_edge = ((near >> 4) & 15) + jnp.where(near < 0, 16, 0)
     near_side = (near < 0) | (near >= 256)
 
-    tail.wait_recv()
+    @pl.when(has_down)
+    def _():
+        tail.wait_recv()
+
     lane = lax.broadcasted_iota(jnp.int32, (64, 128), 1)
-    before = dot(taps[0:128], jnp.where(c > 0, tail_s[...], 0.0))
+    before = dot(taps[0:128], tail_s[...])
     first = (
         zero[:, :128]
         + pltpu.roll(jnp.where(lane == 127, before[64:128], one[:, :128]), 1, 1)
@@ -246,27 +268,40 @@
             (up, prev_s, up_out, up_in, ups),
             (down, next_s, down_out, down_in, downs),
         ):
-            copy = pltpu.make_async_remote_copy(
-                src_ref=pool_s.at[s, :, pl.ds(256, 128)],
-                dst_ref=target.at[s],
-                send_sem=out.at[slot],
-                recv_sem=into.at[slot],
-                device_id=(to, cell_to),
-                device_id_type=MESH,
-            )
+            kept.append(
+                pltpu.make_async_remote_copy(
+                    src_ref=pool_s.at[s, :, pl.ds(256, 128)],
+                    dst_ref=target.at[s],
+                    send_sem=out.at[slot],
+                    recv_sem=into.at[slot],
+                    device_id=(to, cell_to),
+                    device_id_type=MESH,
+                )
+            )
+        if slot:
+            pools.append(
+                pltpu.make_async_remote_copy(
+                    src_ref=pool_s.at[s, :, pl.ds(0, 256)],
+                    dst_ref=pool_s.at[s, :, pl.ds(0, 256)],
+                    send_sem=pool_out.at[slot],
+                    recv_sem=pool_in.at[slot],
+                    device_id=(to, c),
+                    device_id_type=MESH,
+                )
+            )
+
+    @pl.when(has_up)
+    def _():
+        for copy in ups:
             copy.start()
-            kept.append(copy)
-        if slot:
-            copy = pltpu.make_async_remote_copy(
-                src_ref=pool_s.at[s, :, pl.ds(0, 256)],
-                dst_ref=pool_s.at[s, :, pl.ds(0, 256)],
-                send_sem=pool_out.at[slot],
-                recv_sem=pool_in.at[slot],
-                device_id=(to, c),
-                device_id_type=MESH,
-            )
+
+    @pl.when(has_down)
+    def _():
+        for copy in downs:
             copy.start()
-            pools.append(copy)
+
+    for copy in pools:
+        copy.start()
     for copy in pools:
         copy.wait_recv()
     inner = dot(stencil, pool_s[:, :, 0:256].reshape(64, 256))
@@ -286,8 +321,17 @@
                 )
             )
         picked.append(halves)
-    for copy in ups + downs:
-        copy.wait_recv()
+
+    @pl.when(has_down)
+    def _():
+        for copy in ups:
+            copy.wait_recv()
+
+    @pl.when(has_up)
+    def _():
+        for copy in downs:
+            copy.wait_recv()
+
     sides = jnp.where(
         lane < 16, next_s[...].reshape(64, 128), prev_s[...].reshape(64, 128)
     )
@@ -303,8 +347,17 @@
             )
         out_ref[:, h * 128 : (h + 1) * 128] = total
 
-    tail.wait_send()
-    for copy in parts + pools + ups + downs:
+    @pl.when(has_up)
+    def _():
+        for copy in [tail] + ups:
+            copy.wait_send()
+
+    @pl.when(has_down)
+    def _():
+        for copy in downs:
+            copy.wait_send()
+
+    for copy in parts + pools:
         copy.wait_send()
 
 
@@ -314,7 +367,10 @@
     return pl.pallas_call(
         kernel,
         out_shape=jax.ShapeDtypeStruct((8, 256), f32),
-        in_specs=[pl.BlockSpec(memory_space=pltpu.HBM)] * 10,
+        in_specs=[
+            pl.BlockSpec(memory_space=pltpu.SMEM if i == 7 else pltpu.HBM)
+            for i in range(10)
+        ],
         out_specs=pl.BlockSpec(memory_space=pltpu.VMEM),
         scratch_shapes=[
             pltpu.VMEM((64, 512), f32),
@@ -324,7 +380,6 @@
             pltpu.VMEM((64, 256), f32),
             pltpu.VMEM((1, 512), f32),
             pltpu.VMEM((1, 512), i32),
-            pltpu.SMEM((1, 1), i32),
             pltpu.VMEM((8, 256), i32),
             pltpu.VMEM((8, 576), f32),
             pltpu.VMEM((64, 128), f32),
@@ -333,7 +388,7 @@
             pltpu.VMEM((8, 8, 384), f32),
             pltpu.VMEM((8, 8, 128), f32),
             pltpu.VMEM((8, 8, 128), f32),
-            dma((10,)),
+            dma((9,)),
             dma((2,)),
         ]
         + [dma((8,))] * 8,

time: 31.4 us -> 26.4 us (0.84)
  the two profiles are of different devices: /device:TPU:1 before, /device:TPU:185 now
where the time goes in v2:
time: 26.4 us; the launch traced here: 26.2 us
  Pallas kernels  24.3 us (92%)
  local copies, waits for them, and re-layouts  1.3 us (5%)
  between operations  0.66 us (2%)
    pallas_call x1, Pallas kernels, on_device(): pl.pallas_call(kernel, out_shape=jax.ShapeDtypeStruct((8, 256), f32), in_...  24.3 us
    unnamed x1, local copies, waits for them, and re-layouts  1.3 us

profile of v2, /device:TPU:185, one launch (start us, length us, event | category | flops | bytes accessed | tf_op | source)
XLA Modules:
  0.0 26.2 jit_solution(11375631500665325338)
XLA Ops:
  0.7 24.3 %shard_map.100 = f32[8,256]{1,0:T(8,128)} custom-call(f32[1,64,512]{2,1,0:T(8,128)} %swath_ref.1, f32[1,64,192]{2,1,0:T(8,128)} %enc_ref.1, f32[64,64]{1,0:T(8,128)} %key_ref.1, f32[64,64]{1,0:T(8,128)} %value_ref.1, f32[64,256]{1,0:T(8,128)} %query_ref.1, f32[1,512]{1,0:T(1,128)} %quality_ref.1, s32[1,512]{1,0:T(1,128)} %cell_ref.1, ...), custom_call_target="tpu_custom_call" | custom-call | tf_op jit(solution)/shard_map/pallas_call | solution.py:367
  25.0 1.3 %copy.13 = f32[8,256]{1,0:T(8,128)} copy(f32[8,256]{1,0:T(8,128)} %shard_map.100) | data formatting | bytes 16384

commit v3 on v2

--- a/solution.py
+++ b/solution.py
@@ -1,3 +1,5 @@
+import functools
+
 import jax
 import jax.numpy as jnp
 from jax import lax
@@ -25,8 +27,7 @@
     high = x.astype(jnp.bfloat16)
     rest = x - high.astype(jnp.float32)
     mid = rest.astype(jnp.bfloat16)
-    low = (rest - mid.astype(jnp.float32)).astype(jnp.bfloat16)
-    return jnp.concatenate([high, mid, low], axis=0)
+    return high, mid, (rest - mid.astype(jnp.float32)).astype(jnp.bfloat16)
 
 
 def gelu(x):
@@ -55,8 +56,12 @@
     near_s,
     hp_s,
     tail_s,
+    head_s,
     send_s,
+    span_s,
+    edge_s,
     part_s,
+    spans_s,
     pool_s,
     prev_s,
     next_s,
@@ -64,12 +69,15 @@
     tail_sem,
     part_out,
     part_in,
+    span_out,
+    span_in,
     pool_out,
     pool_in,
     up_out,
     up_in,
     down_out,
     down_in,
+    ready,
 ):
     s = lax.axis_index("sensor")
     c = lax.axis_index("cell")
@@ -84,11 +92,11 @@
         pltpu.make_async_copy(source, target, in_sem.at[i])
         for i, (source, target) in enumerate(
             (
+                (swath_ref.at[0], x_s),
                 (cell_ref, cell_s),
                 (query_ref, query_s),
                 (key_ref, key_s),
                 (enc_ref.at[0], enc_s),
-                (swath_ref.at[0], x_s),
                 (quality_ref, quality_s),
                 (hp_ref.at[pl.ds(pl.multiple_of(s * 8, 8), 8)], hp_s),
                 (value_ref, value_s),
@@ -112,12 +120,25 @@
         pl.semaphore_signal(
             barrier, inc=1, device_id=(partner(dz, dx), c), device_id_type=MESH
         )
+    loads[0].wait()
+    last = jnp.transpose(x_s[:, 384:512])
+    row = lax.broadcasted_iota(jnp.int32, (8, 64), 0)
+    head_s[...] = jnp.where(
+        lax.broadcasted_iota(jnp.int32, (8, 128), 0) < 2,
+        jnp.concatenate(
+            [
+                jnp.where(row == 0, last[126:127], last[127:128]),
+                jnp.where(row == 0, last[127:128], 0.0),
+            ],
+            axis=1,
+        ),
+        0.0,
+    )
     pl.semaphore_wait(
         barrier, 7 + has_up.astype(jnp.int32) + has_down.astype(jnp.int32)
     )
-
     tail = pltpu.make_async_remote_copy(
-        src_ref=swath_ref.at[0, :, pl.ds(384, 128)],
+        src_ref=head_s,
         dst_ref=tail_s,
         send_sem=tail_sem.at[0],
         recv_sem=tail_sem.at[1],
@@ -129,16 +150,21 @@
     def _():
         tail.start()
 
+    for dz, dx in OFFSETS:
+        pl.semaphore_signal(
+            ready, inc=1, device_id=(partner(dz, dx), c), device_id_type=MESH
+        )
+
     @pl.when(jnp.logical_not(has_down))
     def _():
-        tail_s[...] = jnp.zeros((64, 128), jnp.float32)
-        prev_s[...] = jnp.zeros((8, 8, 128), jnp.float32)
+        tail_s[...] = jnp.zeros((8, 128), jnp.float32)
+        prev_s[...] = jnp.ones((8, 16, 128), jnp.float32)
 
     @pl.when(jnp.logical_not(has_up))
     def _():
-        next_s[...] = jnp.zeros((8, 8, 128), jnp.float32)
-
-    for i in range(3):
+        next_s[...] = jnp.ones((8, 16, 128), jnp.float32)
+
+    for i in range(1, 4):
         loads[i].wait()
     query = query_s[...]
     bilinear = dot(key_s[...], query, ((0,), (0,))) * 0.125
@@ -156,13 +182,33 @@
         )
     hot = lax.broadcasted_iota(jnp.int32, (256, 512), 0) == cell
 
-    for i in range(3, 6):
+    def edge_cell(shape):
+        row = lax.broadcasted_iota(jnp.int32, shape, 0)
+        return (row & 15) * 16 + jnp.where(row >= 16, 15, 0)
+
+    edge_hot = edge_cell((32, 512)) == cell
+    chosen = edge_cell((32, 256)) == lax.broadcasted_iota(jnp.int32, (32, 256), 1)
+    edge_query = dot(
+        jnp.where(chosen, 1.0, 0.0),
+        jnp.concatenate([query, jnp.ones((64, 256), jnp.float32)], axis=0),
+        ((1,), (1,)),
+    )
+    edge_prior = jnp.max(jnp.where(chosen, prior, FLOOR), axis=1, keepdims=True)
+    edge_prior = jnp.where(s == 0, edge_prior, FLOOR)
+
+    for i in range(4, 6):
         loads[i].wait()
     enc = enc_s[...]
     taps = jnp.concatenate([enc[:, 0:64], enc[:, 64:128], enc[:, 128:192]], axis=0)
     mixed = dot(taps, x_s[...])
     two, one, zero = mixed[0:64], mixed[64:128], mixed[128:192]
     rest = zero + pltpu.roll(one, 1, 1) + pltpu.roll(two, 2, 1)
+    lane = lax.broadcasted_iota(jnp.int32, (64, 128), 1)
+    early = (
+        zero[:, :128]
+        + jnp.where(lane < 1, 0.0, pltpu.roll(one[:, :128], 1, 1))
+        + jnp.where(lane < 2, 0.0, pltpu.roll(two[:, :128], 2, 1))
+    )
     quality = quality_s[...]
     valid = lax.broadcasted_iota(jnp.int32, (1, 512), 1) < live_ref[0, 0]
 
@@ -188,123 +234,145 @@
     def _():
         tail.wait_recv()
 
-    lane = lax.broadcasted_iota(jnp.int32, (64, 128), 1)
-    before = dot(taps[0:128], tail_s[...])
-    first = (
-        zero[:, :128]
-        + pltpu.roll(jnp.where(lane == 127, before[64:128], one[:, :128]), 1, 1)
-        + pltpu.roll(jnp.where(lane >= 126, before[0:64], two[:, :128]), 2, 1)
-    )
+    before = dot(enc[:, 0:128], tail_s[...], ((1,), (1,)))
+    first = early + jnp.concatenate([before, jnp.zeros((64, 120), jnp.float32)], axis=1)
     encoded[0] = gelu(first)
     score[0] = scored(encoded[0], 0)
 
     encoded = jnp.concatenate(encoded, axis=1)
     score = jnp.concatenate(score, axis=1)
-    peak = jnp.max(
-        jnp.where(hot, jnp.where(valid, score, FLOOR), FLOOR), axis=1, keepdims=True
-    )
+    masked = jnp.where(valid, score, FLOOR)
+    peak = jnp.max(jnp.where(hot, masked, FLOOR), axis=1, keepdims=True)
     own_peak = jnp.max(jnp.where(hot, peak, FLOOR), axis=0, keepdims=True)
     weight = jnp.where(valid, jnp.exp(score - own_peak), 0.0)
-    weighted = jnp.concatenate(
-        [encoded * weight, jnp.broadcast_to(weight, (8, 512))], axis=0
-    )
-    sums = dot(
-        split3(weighted),
-        jnp.where(hot, 1.0, 0.0).astype(jnp.bfloat16),
-        ((1,), (1,)),
-        None,
-    )
-    sums = sums[0:72] + (sums[72:144] + sums[144:216])
+    thirds = split3(encoded * weight)
+    weights = split3(jnp.broadcast_to(weight, (8, 512)))
+    one_hot = jnp.where(hot, 1.0, 0.0).astype(jnp.bfloat16)
+    turned = ((1,), (1,))
+    sums = sum(dot(third, one_hot, turned, None) for third in thirds)
+    total = sum(dot(third, one_hot, turned, None) for third in weights)[0:1]
     eye = lax.broadcasted_iota(jnp.int32, (256, 256), 0) == lax.broadcasted_iota(
         jnp.int32, (256, 256), 1
     )
     peak_row = jnp.max(jnp.where(eye, peak, FLOOR), axis=0, keepdims=True)
-    extra = jnp.concatenate([peak_row, sums[64:65]], axis=0)
-    for k in range(8):
-        send_s[k, 0:8] = sums[k * 8 : (k + 1) * 8]
-        send_s[k, 8:10] = extra
+    span = jnp.concatenate([peak_row, total], axis=0)
+    span_s[...] = span
+    send_s[...] = sums.reshape(8, 8, 256)
 
     parts = []
     for dz, dx in OFFSETS:
         slot = dz * 4 + dx
-        copy = pltpu.make_async_remote_copy(
-            src_ref=send_s.at[partner(dz, dx)],
-            dst_ref=part_s.at[slot],
-            send_sem=part_out.at[slot],
-            recv_sem=part_in.at[slot],
-            device_id=(partner(dz, dx), c),
-            device_id_type=MESH,
-        )
-        copy.start()
-        parts.append(copy)
+        to = partner(dz, dx)
+        for source, target, out, into in (
+            (send_s.at[to], part_s.at[slot], part_out, part_in),
+            (span_s, spans_s.at[slot], span_out, span_in),
+        ):
+            copy = pltpu.make_async_remote_copy(
+                src_ref=source,
+                dst_ref=target,
+                send_sem=out.at[slot],
+                recv_sem=into.at[slot],
+                device_id=(to, c),
+                device_id_type=MESH,
+            )
+            copy.start()
+            parts.append(copy)
+
+    edge_peak = jnp.max(jnp.where(edge_hot, masked, FLOOR), axis=1, keepdims=True)
+    edge_one_hot = jnp.where(edge_hot, 1.0, 0.0).astype(jnp.bfloat16)
+    edge_sums = sum(
+        dot(edge_one_hot, jnp.concatenate([third] + [extra] * 8, axis=0), turned, None)
+        for third, extra in zip(thirds, weights)
+    )
+    edge_joint = jnp.maximum(edge_peak, edge_prior)
+    edge_s[...] = jnp.where(
+        lax.broadcasted_iota(jnp.int32, (32, 128), 1) < 96,
+        edge_sums * jnp.exp(edge_peak - edge_joint)
+        + edge_query * jnp.exp(edge_prior - edge_joint),
+        edge_joint,
+    )
+    ups, downs = [], []
+    for dz, dx in OFFSETS + ((0, 0),):
+        slot = dz * 4 + dx
+        for rows, cell_to, target, out, into, kept in (
+            (16, up, prev_s, up_out, up_in, ups),
+            (0, down, next_s, down_out, down_in, downs),
+        ):
+            kept.append(
+                pltpu.make_async_remote_copy(
+                    src_ref=edge_s.at[pl.ds(rows, 16)],
+                    dst_ref=target.at[slot],
+                    send_sem=out.at[slot],
+                    recv_sem=into.at[slot],
+                    device_id=(partner(dz, dx), cell_to),
+                    device_id_type=MESH,
+                )
+            )
+
+    pl.semaphore_wait(ready, 7)
+
+    @pl.when(has_up)
+    def _():
+        for copy in ups:
+            copy.start()
+
+    @pl.when(has_down)
+    def _():
+        for copy in downs:
+            copy.start()
+
     own = send_s[s]
     for copy in parts:
         copy.wait_recv()
     blocks = [own] + [part_s[k] for k in range(1, 8)]
-    peaks = jnp.concatenate([block[8:9] for block in blocks], axis=0)
-    totals = jnp.concatenate([block[9:10] for block in blocks], axis=0)
+    spans = [span] + [spans_s[k] for k in range(1, 8)]
+    peaks = jnp.concatenate([one[0:1] for one in spans], axis=0)
+    totals = jnp.concatenate([one[1:2] for one in spans], axis=0)
     joint = jnp.maximum(jnp.max(peaks, axis=0, keepdims=True), prior)
     factor = jnp.exp(peaks - joint)
     prior_factor = jnp.exp(prior - joint)
     below = jnp.sum(totals * factor, axis=0, keepdims=True) + prior_factor
     above = query_s[pl.ds(pl.multiple_of(s * 8, 8), 8), :] * prior_factor
     for k in range(8):
-        above = above + blocks[k][0:8] * factor[k : k + 1]
-    pooled = above / below
-    edge = lax.broadcasted_iota(jnp.int32, (8, 128), 1)
-    edge_cell = (edge & 15) * 16 + jnp.where((edge & 16) > 0, 15, 0)
-    pool_s[s, :, 0:256] = pooled
-    pool_s[s, :, 256:384] = jnp.where(
-        edge_cell >= 128,
-        lanes(pooled[:, 128:], edge_cell & 127),
-        lanes(pooled[:, :128], edge_cell & 127),
-    )
-
-    ups, downs, pools = [], [], []
-    for dz, dx in OFFSETS + ((0, 0),):
+        above = above + blocks[k] * factor[k : k + 1]
+    pool_s[s] = above / below
+
+    pools = []
+    for dz, dx in OFFSETS:
         slot = dz * 4 + dx
-        to = partner(dz, dx)
-        for cell_to, target, out, into, kept in (
-            (up, prev_s, up_out, up_in, ups),
-            (down, next_s, down_out, down_in, downs),
-        ):
-            kept.append(
-                pltpu.make_async_remote_copy(
-                    src_ref=pool_s.at[s, :, pl.ds(256, 128)],
-                    dst_ref=target.at[s],
-                    send_sem=out.at[slot],
-                    recv_sem=into.at[slot],
-                    device_id=(to, cell_to),
-                    device_id_type=MESH,
-                )
-            )
-        if slot:
-            pools.append(
-                pltpu.make_async_remote_copy(
-                    src_ref=pool_s.at[s, :, pl.ds(0, 256)],
-                    dst_ref=pool_s.at[s, :, pl.ds(0, 256)],
-                    send_sem=pool_out.at[slot],
-                    recv_sem=pool_in.at[slot],
-                    device_id=(to, c),
-                    device_id_type=MESH,
-                )
-            )
+        copy = pltpu.make_async_remote_copy(
+            src_ref=pool_s.at[s],
+            dst_ref=pool_s.at[s],
+            send_sem=pool_out.at[slot],
+            recv_sem=pool_in.at[slot],
+            device_id=(partner(dz, dx), c),
+            device_id_type=MESH,
+        )
+        copy.start()
+        pools.append(copy)
+
+    @pl.when(has_down)
+    def _():
+        for copy in ups:
+            copy.wait_recv()
 
     @pl.when(has_up)
     def _():
-        for copy in ups:
-            copy.start()
-
-    @pl.when(has_down)
-    def _():
         for copy in downs:
-            copy.start()
-
-    for copy in pools:
-        copy.start()
+            copy.wait_recv()
+
+    edges = []
+    for side in (next_s, prev_s):
+        blocks = [side[k] for k in range(8)]
+        joint = functools.reduce(jnp.maximum, blocks)[:, 96:97]
+        whole = sum(block * jnp.exp(block[:, 96:97] - joint) for block in blocks)
+        edges.append(whole[:, 0:64] / whole[:, 64:65])
+    edges = jnp.concatenate(edges + [jnp.zeros((96, 64), jnp.float32)], axis=0)
+    outer = dot(stencil[8:72], edges, turned)
+
     for copy in pools:
         copy.wait_recv()
-    inner = dot(stencil, pool_s[:, :, 0:256].reshape(64, 256))
+    inner = dot(stencil, pool_s[...].reshape(64, 256))
     joined = inner[0:8]
     picked = []
     for k in range(8):
@@ -322,20 +390,6 @@
             )
         picked.append(halves)
 
-    @pl.when(has_down)
-    def _():
-        for copy in ups:
-            copy.wait_recv()
-
-    @pl.when(has_up)
-    def _():
-        for copy in downs:
-            copy.wait_recv()
-
-    sides = jnp.where(
-        lane < 16, next_s[...].reshape(64, 128), prev_s[...].reshape(64, 128)
-    )
-    outer = dot(stencil[8:72], sides)
     for h in range(2):
         total = joined[:, h * 128 : (h + 1) * 128]
         for k in range(8):
@@ -382,16 +436,21 @@
             pltpu.VMEM((1, 512), i32),
             pltpu.VMEM((8, 256), i32),
             pltpu.VMEM((8, 576), f32),
-            pltpu.VMEM((64, 128), f32),
-            pltpu.VMEM((8, 10, 256), f32),
-            pltpu.VMEM((8, 10, 256), f32),
-            pltpu.VMEM((8, 8, 384), f32),
-            pltpu.VMEM((8, 8, 128), f32),
-            pltpu.VMEM((8, 8, 128), f32),
+            pltpu.VMEM((8, 128), f32),
+            pltpu.VMEM((8, 128), f32),
+            pltpu.VMEM((8, 8, 256), f32),
+            pltpu.VMEM((2, 256), f32),
+            pltpu.VMEM((32, 128), f32),
+            pltpu.VMEM((8, 8, 256), f32),
+            pltpu.VMEM((8, 2, 256), f32),
+            pltpu.VMEM((8, 8, 256), f32),
+            pltpu.VMEM((8, 16, 128), f32),
+            pltpu.VMEM((8, 16, 128), f32),
             dma((9,)),
             dma((2,)),
         ]
-        + [dma((8,))] * 8,
+        + [dma((8,))] * 10
+        + [pltpu.SemaphoreType.REGULAR],
         compiler_params=pltpu.CompilerParams(collective_id=0, has_side_effects=True),
     )(*operands)
 

time: 26.4 us -> 23.1 us (0.88)
  Pallas kernels: 24.3 us -> 21 us
    pallas_call x1, Pallas kernels: 24.3 us -> 21 us  [on_device(): pl.pallas_call(kernel, out_shape=jax.ShapeDtypeStruct((8, 256), f32), in_...]
where the time goes in v3:
time: 23.1 us; the launch traced here: 22.9 us
  Pallas kernels  21 us (91%)
  local copies, waits for them, and re-layouts  1.3 us (6%)
  between operations  0.66 us (3%)
    pallas_call x1, Pallas kernels, on_device(): pl.pallas_call(kernel, out_shape=jax.ShapeDtypeStruct((8, 256), f32), in_...  21 us
    unnamed x1, local copies, waits for them, and re-layouts  1.3 us

profile of v3, /device:TPU:185, one launch (start us, length us, event | category | flops | bytes accessed | tf_op | source)
XLA Modules:
  0.0 22.9 jit_solution(13387907559377552006)
XLA Ops:
  0.7 21.0 %shard_map.100 = f32[8,256]{1,0:T(8,128)} custom-call(f32[1,64,512]{2,1,0:T(8,128)} %swath_ref.1, f32[1,64,192]{2,1,0:T(8,128)} %enc_ref.1, f32[64,64]{1,0:T(8,128)} %key_ref.1, f32[64,64]{1,0:T(8,128)} %value_ref.1, f32[64,256]{1,0:T(8,128)} %query_ref.1, f32[1,512]{1,0:T(1,128)} %quality_ref.1, s32[1,512]{1,0:T(1,128)} %cell_ref.1, ...), custom_call_target="tpu_custom_call" | custom-call | tf_op jit(solution)/shard_map/pallas_call | solution.py:421
  21.6 1.3 %copy.13 = f32[8,256]{1,0:T(8,128)} copy(f32[8,256]{1,0:T(8,128)} %shard_map.100) | data formatting | bytes 16384

commit v4 on v3

--- a/solution.py
+++ b/solution.py
@@ -9,7 +9,7 @@
 
 MESH = pl.DeviceIdType.MESH
 FLOOR = -1e30
-HIGHEST = lax.Precision.HIGHEST
+HIGH, HIGHEST = lax.Precision.HIGH, lax.Precision.HIGHEST
 OFFSETS = ((1, 2), (0, 2), (1, 1), (1, 3), (0, 1), (0, 3), (1, 0))
 
 
@@ -21,13 +21,6 @@
 
 def lanes(values, index):
     return jnp.take_along_axis(values, index, axis=1, mode="promise_in_bounds")
-
-
-def split3(x):
-    high = x.astype(jnp.bfloat16)
-    rest = x - high.astype(jnp.float32)
-    mid = rest.astype(jnp.bfloat16)
-    return high, mid, (rest - mid.astype(jnp.float32)).astype(jnp.bfloat16)
 
 
 def gelu(x):
@@ -55,6 +48,7 @@
     cell_s,
     near_s,
     hp_s,
+    mixed_s,
     tail_s,
     head_s,
     send_s,
@@ -120,7 +114,8 @@
         pl.semaphore_signal(
             barrier, inc=1, device_id=(partner(dz, dx), c), device_id_type=MESH
         )
-    loads[0].wait()
+    for i in range(6):
+        loads[i].wait()
     last = jnp.transpose(x_s[:, 384:512])
     row = lax.broadcasted_iota(jnp.int32, (8, 64), 0)
     head_s[...] = jnp.where(
@@ -134,6 +129,14 @@
         ),
         0.0,
     )
+
+    query = query_s[...]
+    bilinear = dot(key_s[...], query, ((0,), (0,))) * 0.125
+    enc = enc_s[...]
+    taps = jnp.concatenate([enc[:, 0:64], enc[:, 64:128], enc[:, 128:192]], axis=0)
+    mixed = dot(taps, x_s[...])
+    mixed_s[...] = mixed
+
     pl.semaphore_wait(
         barrier, 7 + has_up.astype(jnp.int32) + has_down.astype(jnp.int32)
     )
@@ -164,11 +167,15 @@
     def _():
         next_s[...] = jnp.ones((8, 16, 128), jnp.float32)
 
-    for i in range(1, 4):
-        loads[i].wait()
-    query = query_s[...]
-    bilinear = dot(key_s[...], query, ((0,), (0,))) * 0.125
-    prior = jnp.sum(query * bilinear, axis=0, keepdims=True)
+    mixed = mixed_s[...]
+    two, one, zero = mixed[0:64], mixed[64:128], mixed[128:192]
+    slot = lax.broadcasted_iota(jnp.int32, (1, 512), 1)
+    drawn = (
+        zero
+        + jnp.where(slot < 1, 0.0, pltpu.roll(one, 1, 1))
+        + jnp.where(slot < 2, 0.0, pltpu.roll(two, 2, 1))
+    )
+    encoded = gelu(drawn)
     cell = cell_s[...]
     asked = []
     for b in range(4):
@@ -180,82 +187,65 @@
                 lanes(bilinear[:, :128], index & 127),
             )
         )
+    quality = quality_s[...]
+    live = live_ref[0, 0]
+    score = jnp.sum(encoded * jnp.concatenate(asked, axis=1), axis=0, keepdims=True)
+    score = score + quality
+    valid = (slot < live) & (slot >= 2)
+
     hot = lax.broadcasted_iota(jnp.int32, (256, 512), 0) == cell
-
-    def edge_cell(shape):
-        row = lax.broadcasted_iota(jnp.int32, shape, 0)
-        return (row & 15) * 16 + jnp.where(row >= 16, 15, 0)
-
-    edge_hot = edge_cell((32, 512)) == cell
-    chosen = edge_cell((32, 256)) == lax.broadcasted_iota(jnp.int32, (32, 256), 1)
-    edge_query = dot(
-        jnp.where(chosen, 1.0, 0.0),
-        jnp.concatenate([query, jnp.ones((64, 256), jnp.float32)], axis=0),
-        ((1,), (1,)),
-    )
-    edge_prior = jnp.max(jnp.where(chosen, prior, FLOOR), axis=1, keepdims=True)
-    edge_prior = jnp.where(s == 0, edge_prior, FLOOR)
-
-    for i in range(4, 6):
-        loads[i].wait()
-    enc = enc_s[...]
-    taps = jnp.concatenate([enc[:, 0:64], enc[:, 64:128], enc[:, 128:192]], axis=0)
-    mixed = dot(taps, x_s[...])
-    two, one, zero = mixed[0:64], mixed[64:128], mixed[128:192]
-    rest = zero + pltpu.roll(one, 1, 1) + pltpu.roll(two, 2, 1)
-    lane = lax.broadcasted_iota(jnp.int32, (64, 128), 1)
-    early = (
-        zero[:, :128]
-        + jnp.where(lane < 1, 0.0, pltpu.roll(one[:, :128], 1, 1))
-        + jnp.where(lane < 2, 0.0, pltpu.roll(two[:, :128], 2, 1))
-    )
-    quality = quality_s[...]
-    valid = lax.broadcasted_iota(jnp.int32, (1, 512), 1) < live_ref[0, 0]
-
-    def scored(encoded, b):
-        return (
-            jnp.sum(encoded * asked[b], axis=0, keepdims=True)
-            + quality[:, b * 128 : (b + 1) * 128]
-        )
-
-    encoded = [None] + [gelu(rest[:, b * 128 : (b + 1) * 128]) for b in range(1, 4)]
-    score = [None] + [scored(encoded[b], b) for b in range(1, 4)]
-
-    for i in range(6, 9):
-        loads[i].wait()
-    hp = hp_s[...]
-    stacked = jnp.concatenate([hp[:, k * 64 : (k + 1) * 64] for k in range(9)], axis=0)
-    stencil = dot(stacked, value_s[...])
-    near = near_s[...] - c * 256
-    near_edge = ((near >> 4) & 15) + jnp.where(near < 0, 16, 0)
-    near_side = (near < 0) | (near >= 256)
-
-    @pl.when(has_down)
-    def _():
-        tail.wait_recv()
-
-    before = dot(enc[:, 0:128], tail_s[...], ((1,), (1,)))
-    first = early + jnp.concatenate([before, jnp.zeros((64, 120), jnp.float32)], axis=1)
-    encoded[0] = gelu(first)
-    score[0] = scored(encoded[0], 0)
-
-    encoded = jnp.concatenate(encoded, axis=1)
-    score = jnp.concatenate(score, axis=1)
     masked = jnp.where(valid, score, FLOOR)
     peak = jnp.max(jnp.where(hot, masked, FLOOR), axis=1, keepdims=True)
-    own_peak = jnp.max(jnp.where(hot, peak, FLOOR), axis=0, keepdims=True)
-    weight = jnp.where(valid, jnp.exp(score - own_peak), 0.0)
-    thirds = split3(encoded * weight)
-    weights = split3(jnp.broadcast_to(weight, (8, 512)))
+    slot_peak = jnp.max(jnp.where(hot, peak, FLOOR), axis=0, keepdims=True)
+    weight = jnp.where(valid, jnp.exp(score - slot_peak), 0.0)
+    weighted = jnp.concatenate(
+        [encoded * weight, jnp.broadcast_to(weight, (8, 512))], axis=0
+    )
     one_hot = jnp.where(hot, 1.0, 0.0).astype(jnp.bfloat16)
     turned = ((1,), (1,))
-    sums = sum(dot(third, one_hot, turned, None) for third in thirds)
-    total = sum(dot(third, one_hot, turned, None) for third in weights)[0:1]
+    high = weighted.astype(jnp.bfloat16)
+    low = (weighted - high.astype(jnp.float32)).astype(jnp.bfloat16)
+    sums = dot(high, one_hot, turned, None) + dot(low, one_hot, turned, None)
     eye = lax.broadcasted_iota(jnp.int32, (256, 256), 0) == lax.broadcasted_iota(
         jnp.int32, (256, 256), 1
     )
-    peak_row = jnp.max(jnp.where(eye, peak, FLOOR), axis=0, keepdims=True)
-    span = jnp.concatenate([peak_row, total], axis=0)
+    peak = jnp.max(jnp.where(eye, peak, FLOOR), axis=0, keepdims=True)
+    prior = jnp.sum(query * bilinear, axis=0, keepdims=True)
+    prior = jnp.where(s == 0, prior, FLOOR)
+    joint = jnp.maximum(peak, prior)
+    factor = jnp.exp(peak - joint)
+    prior_factor = jnp.exp(prior - joint)
+    total = sums[64:65] * factor + prior_factor
+    sums = sums[0:64] * factor + query * prior_factor
+    peak = joint
+
+    @pl.when(has_down)
+    def _():
+        tail.wait_recv()
+
+    before = dot(enc[:, 0:128], tail_s[...], turned)
+    first = gelu(
+        drawn[:, 0:128]
+        + jnp.concatenate([before, jnp.zeros((64, 120), jnp.float32)], axis=1)
+    )
+    first_score = jnp.sum(first * asked[0], axis=0, keepdims=True) + quality[:, 0:128]
+    cells = lax.broadcasted_iota(jnp.int32, (1, 256), 1)
+    scores = [
+        jnp.where(
+            (cells == cell[:, t : t + 1]) & (t < live), first_score[:, t : t + 1], FLOOR
+        )
+        for t in range(2)
+    ]
+    joint = jnp.maximum(peak, jnp.maximum(scores[0], scores[1]))
+    factor = jnp.exp(peak - joint)
+    total, sums = total * factor, sums * factor
+    for t in range(2):
+        weight = jnp.where(
+            (cells == cell[:, t : t + 1]) & (t < live), jnp.exp(scores[t] - joint), 0.0
+        )
+        total = total + weight
+        sums = sums + first[:, t : t + 1] * weight
+    span = jnp.concatenate([joint, total], axis=0)
     span_s[...] = span
     send_s[...] = sums.reshape(8, 8, 256)
 
@@ -278,18 +268,14 @@
             copy.start()
             parts.append(copy)
 
-    edge_peak = jnp.max(jnp.where(edge_hot, masked, FLOOR), axis=1, keepdims=True)
-    edge_one_hot = jnp.where(edge_hot, 1.0, 0.0).astype(jnp.bfloat16)
-    edge_sums = sum(
-        dot(edge_one_hot, jnp.concatenate([third] + [extra] * 8, axis=0), turned, None)
-        for third, extra in zip(thirds, weights)
-    )
-    edge_joint = jnp.maximum(edge_peak, edge_prior)
-    edge_s[...] = jnp.where(
-        lax.broadcasted_iota(jnp.int32, (32, 128), 1) < 96,
-        edge_sums * jnp.exp(edge_peak - edge_joint)
-        + edge_query * jnp.exp(edge_prior - edge_joint),
-        edge_joint,
+    row = lax.broadcasted_iota(jnp.int32, (32, 256), 0)
+    chosen = lax.broadcasted_iota(jnp.int32, (32, 256), 1) == (
+        (row & 15) * 16 + jnp.where(row >= 16, 15, 0)
+    )
+    edge_s[...] = dot(
+        jnp.where(chosen, 1.0, 0.0),
+        jnp.concatenate([sums, span, jnp.zeros((62, 256), jnp.float32)], axis=0),
+        turned,
     )
     ups, downs = [], []
     for dz, dx in OFFSETS + ((0, 0),):
@@ -308,7 +294,6 @@
                     device_id_type=MESH,
                 )
             )
-
     pl.semaphore_wait(ready, 7)
 
     @pl.when(has_up)
@@ -320,6 +305,15 @@
     def _():
         for copy in downs:
             copy.start()
+
+    for i in range(6, 9):
+        loads[i].wait()
+    hp = hp_s[...]
+    stacked = jnp.concatenate([hp[:, k * 64 : (k + 1) * 64] for k in range(9)], axis=0)
+    stencil = dot(stacked, value_s[...])
+    near = near_s[...] - c * 256
+    near_edge = ((near >> 4) & 15) + jnp.where(near < 0, 16, 0)
+    near_side = (near < 0) | (near >= 256)
 
     own = send_s[s]
     for copy in parts:
@@ -328,13 +322,9 @@
     spans = [span] + [spans_s[k] for k in range(1, 8)]
     peaks = jnp.concatenate([one[0:1] for one in spans], axis=0)
     totals = jnp.concatenate([one[1:2] for one in spans], axis=0)
-    joint = jnp.maximum(jnp.max(peaks, axis=0, keepdims=True), prior)
-    factor = jnp.exp(peaks - joint)
-    prior_factor = jnp.exp(prior - joint)
-    below = jnp.sum(totals * factor, axis=0, keepdims=True) + prior_factor
-    above = query_s[pl.ds(pl.multiple_of(s * 8, 8), 8), :] * prior_factor
-    for k in range(8):
-        above = above + blocks[k] * factor[k : k + 1]
+    factor = jnp.exp(peaks - jnp.max(peaks, axis=0, keepdims=True))
+    below = jnp.sum(totals * factor, axis=0, keepdims=True)
+    above = sum(blocks[k] * factor[k : k + 1] for k in range(8))
     pool_s[s] = above / below
 
     pools = []
@@ -364,15 +354,15 @@
     edges = []
     for side in (next_s, prev_s):
         blocks = [side[k] for k in range(8)]
-        joint = functools.reduce(jnp.maximum, blocks)[:, 96:97]
-        whole = sum(block * jnp.exp(block[:, 96:97] - joint) for block in blocks)
-        edges.append(whole[:, 0:64] / whole[:, 64:65])
+        joint = functools.reduce(jnp.maximum, blocks)[:, 64:65]
+        whole = sum(block * jnp.exp(block[:, 64:65] - joint) for block in blocks)
+        edges.append(whole[:, 0:64] / whole[:, 65:66])
     edges = jnp.concatenate(edges + [jnp.zeros((96, 64), jnp.float32)], axis=0)
-    outer = dot(stencil[8:72], edges, turned)
+    outer = dot(stencil[8:72], edges, turned, HIGH)
 
     for copy in pools:
         copy.wait_recv()
-    inner = dot(stencil, pool_s[...].reshape(64, 256))
+    inner = dot(stencil, pool_s[...].reshape(64, 256), precision=HIGH)
     joined = inner[0:8]
     picked = []
     for k in range(8):
@@ -436,6 +426,7 @@
             pltpu.VMEM((1, 512), i32),
             pltpu.VMEM((8, 256), i32),
             pltpu.VMEM((8, 576), f32),
+            pltpu.VMEM((192, 512), f32),
             pltpu.VMEM((8, 128), f32),
             pltpu.VMEM((8, 128), f32),
             pltpu.VMEM((8, 8, 256), f32),

time: 23.1 us -> 22.4 us (0.970)
  Pallas kernels: 21 us -> 20.3 us
    pallas_call x1, Pallas kernels: 21 us -> 20.3 us  [on_device(): pl.pallas_call(kernel, out_shape=jax.ShapeDtypeStruct((8, 256), f32), in_...]
where the time goes in v4:
time: 22.4 us; the launch traced here: 22.2 us
  Pallas kernels  20.3 us (91%)
  local copies, waits for them, and re-layouts  1.3 us (6%)
  between operations  0.66 us (3%)
    pallas_call x1, Pallas kernels, on_device(): pl.pallas_call(kernel, out_shape=jax.ShapeDtypeStruct((8, 256), f32), in_...  20.3 us
    unnamed x1, local copies, waits for them, and re-layouts  1.3 us

profile of v4, /device:TPU:185, one launch (start us, length us, event | category | flops | bytes accessed | tf_op | source)
XLA Modules:
  0.0 22.2 jit_solution(5168824773070945738)
XLA Ops:
  0.7 20.3 %shard_map.100 = f32[8,256]{1,0:T(8,128)} custom-call(f32[1,64,512]{2,1,0:T(8,128)} %swath_ref.1, f32[1,64,192]{2,1,0:T(8,128)} %enc_ref.1, f32[64,64]{1,0:T(8,128)} %key_ref.1, f32[64,64]{1,0:T(8,128)} %value_ref.1, f32[64,256]{1,0:T(8,128)} %query_ref.1, f32[1,512]{1,0:T(1,128)} %quality_ref.1, s32[1,512]{1,0:T(1,128)} %cell_ref.1, ...), custom_call_target="tpu_custom_call" | custom-call | tf_op jit(solution)/shard_map/pallas_call | solution.py:411
  21.0 1.3 %copy.13 = f32[8,256]{1,0:T(8,128)} copy(f32[8,256]{1,0:T(8,128)} %shard_map.100) | data formatting | bytes 16384

commit v5 on v4

--- a/solution.py
+++ b/solution.py
@@ -21,6 +21,20 @@
 
 def lanes(values, index):
     return jnp.take_along_axis(values, index, axis=1, mode="promise_in_bounds")
+
+
+def split3(x):
+    high = x.astype(jnp.bfloat16).astype(jnp.float32)
+    mid = (x - high).astype(jnp.bfloat16).astype(jnp.float32)
+    return high, mid, x - high - mid
+
+
+def full_dot(a, b):
+    a0, a1, a2 = split3(a)
+    b0, b1, b2 = split3(b)
+    left = jnp.concatenate([a0, a0, a1, a1, a0, a2], axis=1).astype(jnp.bfloat16)
+    right = jnp.concatenate([b0, b1, b0, b1, b2, b0], axis=0).astype(jnp.bfloat16)
+    return dot(left, right, precision=None)
 
 
 def gelu(x):
@@ -49,6 +63,9 @@
     near_s,
     hp_s,
     mixed_s,
+    hot_s,
+    asked_s,
+    prior_s,
     tail_s,
     head_s,
     send_s,
@@ -131,11 +148,22 @@
     )
 
     query = query_s[...]
-    bilinear = dot(key_s[...], query, ((0,), (0,))) * 0.125
+    bilinear = full_dot(jnp.transpose(key_s[...]) * 0.125, query)
+    cell = cell_s[...]
+    hot_s[...] = jnp.where(
+        lax.broadcasted_iota(jnp.int32, (256, 512), 0) == cell, 1.0, 0.0
+    ).astype(jnp.bfloat16)
     enc = enc_s[...]
     taps = jnp.concatenate([enc[:, 0:64], enc[:, 64:128], enc[:, 128:192]], axis=0)
-    mixed = dot(taps, x_s[...])
-    mixed_s[...] = mixed
+    mixed_s[...] = full_dot(taps, x_s[...])
+    for b in range(4):
+        index = jnp.broadcast_to(cell[:, b * 128 : (b + 1) * 128], (64, 128))
+        asked_s[:, b * 128 : (b + 1) * 128] = jnp.where(
+            index >= 128,
+            lanes(bilinear[:, 128:], index & 127),
+            lanes(bilinear[:, :128], index & 127),
+        )
+    prior_s[...] = jnp.sum(query * bilinear, axis=0, keepdims=True)
 
     pl.semaphore_wait(
         barrier, 7 + has_up.astype(jnp.int32) + has_down.astype(jnp.int32)
@@ -177,40 +205,42 @@
     )
     encoded = gelu(drawn)
     cell = cell_s[...]
-    asked = []
-    for b in range(4):
-        index = jnp.broadcast_to(cell[:, b * 128 : (b + 1) * 128], (64, 128))
-        asked.append(
-            jnp.where(
-                index >= 128,
-                lanes(bilinear[:, 128:], index & 127),
-                lanes(bilinear[:, :128], index & 127),
-            )
-        )
     quality = quality_s[...]
     live = live_ref[0, 0]
-    score = jnp.sum(encoded * jnp.concatenate(asked, axis=1), axis=0, keepdims=True)
+    score = jnp.sum(encoded * asked_s[...], axis=0, keepdims=True)
     score = score + quality
     valid = (slot < live) & (slot >= 2)
 
     hot = lax.broadcasted_iota(jnp.int32, (256, 512), 0) == cell
     masked = jnp.where(valid, score, FLOOR)
     peak = jnp.max(jnp.where(hot, masked, FLOOR), axis=1, keepdims=True)
-    slot_peak = jnp.max(jnp.where(hot, peak, FLOOR), axis=0, keepdims=True)
+    eye = lax.broadcasted_iota(jnp.int32, (128, 128), 0) == lax.broadcasted_iota(
+        jnp.int32, (128, 128), 1
+    )
+    halves = [
+        jnp.max(
+            jnp.where(eye, peak[h * 128 : (h + 1) * 128], FLOOR), axis=0, keepdims=True
+        )
+        for h in range(2)
+    ]
+    slot_peak = []
+    for b in range(4):
+        index = jnp.broadcast_to(cell[:, b * 128 : (b + 1) * 128], (8, 128))
+        low, high = (lanes(jnp.broadcast_to(half, (8, 128)), index & 127) for half in halves)
+        slot_peak.append(jnp.where(index >= 128, high, low)[0:1])
+    slot_peak = jnp.concatenate(slot_peak, axis=1)
+    peak = jnp.concatenate(halves, axis=1)
     weight = jnp.where(valid, jnp.exp(score - slot_peak), 0.0)
     weighted = jnp.concatenate(
         [encoded * weight, jnp.broadcast_to(weight, (8, 512))], axis=0
     )
-    one_hot = jnp.where(hot, 1.0, 0.0).astype(jnp.bfloat16)
+    one_hot = hot_s[...]
     turned = ((1,), (1,))
     high = weighted.astype(jnp.bfloat16)
     low = (weighted - high.astype(jnp.float32)).astype(jnp.bfloat16)
     sums = dot(high, one_hot, turned, None) + dot(low, one_hot, turned, None)
-    eye = lax.broadcasted_iota(jnp.int32, (256, 256), 0) == lax.broadcasted_iota(
-        jnp.int32, (256, 256), 1
-    )
-    peak = jnp.max(jnp.where(eye, peak, FLOOR), axis=0, keepdims=True)
-    prior = jnp.sum(query * bilinear, axis=0, keepdims=True)
+    query = query_s[...]
+    prior = prior_s[...]
     prior = jnp.where(s == 0, prior, FLOOR)
     joint = jnp.maximum(peak, prior)
     factor = jnp.exp(peak - joint)
@@ -223,28 +253,29 @@
     def _():
         tail.wait_recv()
 
-    before = dot(enc[:, 0:128], tail_s[...], turned)
-    first = gelu(
-        drawn[:, 0:128]
-        + jnp.concatenate([before, jnp.zeros((64, 120), jnp.float32)], axis=1)
-    )
-    first_score = jnp.sum(first * asked[0], axis=0, keepdims=True) + quality[:, 0:128]
+    parity = (lax.broadcasted_iota(jnp.int32, (64, 128), 1) & 1) == 0
+    late = [
+        jnp.sum(enc_s[:, 0:128] * tail_s[t : t + 1], axis=1, keepdims=True)
+        + drawn[:, t : t + 1]
+        for t in range(2)
+    ]
+    late = gelu(jnp.where(parity, late[0], late[1]))
+    late_score = jnp.sum(
+        late * jnp.where(parity, asked_s[:, 0:1], asked_s[:, 1:2]), axis=0, keepdims=True
+    )
     cells = lax.broadcasted_iota(jnp.int32, (1, 256), 1)
+    there = [(cells == cell[:, t : t + 1]) & (t < live) for t in range(2)]
     scores = [
-        jnp.where(
-            (cells == cell[:, t : t + 1]) & (t < live), first_score[:, t : t + 1], FLOOR
-        )
+        jnp.where(there[t], late_score[:, t : t + 1] + quality[:, t : t + 1], FLOOR)
         for t in range(2)
     ]
     joint = jnp.maximum(peak, jnp.maximum(scores[0], scores[1]))
     factor = jnp.exp(peak - joint)
     total, sums = total * factor, sums * factor
     for t in range(2):
-        weight = jnp.where(
-            (cells == cell[:, t : t + 1]) & (t < live), jnp.exp(scores[t] - joint), 0.0
-        )
+        weight = jnp.where(there[t], jnp.exp(scores[t] - joint), 0.0)
         total = total + weight
-        sums = sums + first[:, t : t + 1] * weight
+        sums = sums + late[:, t : t + 1] * weight
     span = jnp.concatenate([joint, total], axis=0)
     span_s[...] = span
     send_s[...] = sums.reshape(8, 8, 256)
@@ -311,6 +342,8 @@
     hp = hp_s[...]
     stacked = jnp.concatenate([hp[:, k * 64 : (k + 1) * 64] for k in range(9)], axis=0)
     stencil = dot(stacked, value_s[...])
+    part0, part1, _ = split3(stencil)
+    stencil_parts = jnp.concatenate([part0, part1, part0], axis=1).astype(jnp.bfloat16)
     near = near_s[...] - c * 256
     near_edge = ((near >> 4) & 15) + jnp.where(near < 0, 16, 0)
     near_side = (near < 0) | (near >= 256)
@@ -362,7 +395,12 @@
 
     for copy in pools:
         copy.wait_recv()
-    inner = dot(stencil, pool_s[...].reshape(64, 256), precision=HIGH)
+    part0, part1, _ = split3(pool_s[...].reshape(64, 256))
+    inner = dot(
+        stencil_parts,
+        jnp.concatenate([part0, part0, part1], axis=0).astype(jnp.bfloat16),
+        precision=None,
+    )
     joined = inner[0:8]
     picked = []
     for k in range(8):
@@ -410,7 +448,7 @@
     dma = pltpu.SemaphoreType.DMA
     return pl.pallas_call(
         kernel,
-        out_shape=jax.ShapeDtypeStruct((8, 256), f32),
+        out_shape=pltpu.VMEM((8, 256), f32),
         in_specs=[
             pl.BlockSpec(memory_space=pltpu.SMEM if i == 7 else pltpu.HBM)
             for i in range(10)
@@ -427,6 +465,9 @@
             pltpu.VMEM((8, 256), i32),
             pltpu.VMEM((8, 576), f32),
             pltpu.VMEM((192, 512), f32),
+            pltpu.VMEM((256, 512), jnp.bfloat16),
+            pltpu.VMEM((64, 512), f32),
+            pltpu.VMEM((1, 256), f32),
             pltpu.VMEM((8, 128), f32),
             pltpu.VMEM((8, 128), f32),
             pltpu.VMEM((8, 8, 256), f32),

time: 22.4 us -> 21.1 us (0.942)
  local copies, waits for them, and re-layouts: 1.3 us -> 0.6 us
  Pallas kernels: 20.3 us -> 19.7 us
    unnamed x1, local copies, waits for them, and re-layouts: 1.3 us -> 0.6 us
    pallas_call x1, Pallas kernels: 20.3 us -> 19.7 us  [on_device(): pl.pallas_call(kernel, out_shape=pltpu.VMEM((8, 256), f32), in_specs=[pl....]
where the time goes in v5:
time: 21.1 us; the launch traced here: 21 us
  Pallas kernels  19.7 us (93%)
  between operations  0.66 us (3%)
  local copies, waits for them, and re-layouts  0.6 us (3%)
    pallas_call x1, Pallas kernels, on_device(): pl.pallas_call(kernel, out_shape=pltpu.VMEM((8, 256), f32), in_specs=[pl....  19.7 us
    unnamed x1, local copies, waits for them, and re-layouts  0.6 us

profile of v5, /device:TPU:185, one launch (start us, length us, event | category | flops | bytes accessed | tf_op | source)
XLA Modules:
  0.0 21.0 jit_solution(176564220792477226)
XLA Ops:
  0.7 19.7 %shard_map.100 = f32[8,256]{1,0:T(8,128)S(1)} custom-call(f32[1,64,512]{2,1,0:T(8,128)} %swath_ref.1, f32[1,64,192]{2,1,0:T(8,128)} %enc_ref.1, f32[64,64]{1,0:T(8,128)} %key_ref.1, f32[64,64]{1,0:T(8,128)} %value_ref.1, f32[64,256]{1,0:T(8,128)} %query_ref.1, f32[1,512]{1,0:T(1,128)} %quality_ref.1, s32[1,512]{1,0:T(1,128)} %cell_ref.1, ...), custom_call_target="tpu_custom_call" | custom-call | tf_op jit(solution)/shard_map/pallas_call | solution.py:449
  20.4 0.6 %copy.12 = f32[8,256]{1,0:T(8,128)} copy(f32[8,256]{1,0:T(8,128)S(1)} %shard_map.100) | data formatting | bytes 16384

commit v6 on v5

--- a/solution.py
+++ b/solution.py
@@ -71,6 +71,12 @@
     send_s,
     span_s,
     edge_s,
+    early_s,
+    pack_s,
+    packed_s,
+    token_s,
+    tokens_s,
+    side_s,
     part_s,
     spans_s,
     pool_s,
@@ -88,6 +94,9 @@
     up_in,
     down_out,
     down_in,
+    packet_sem,
+    token_out,
+    token_in,
     ready,
 ):
     s = lax.axis_index("sensor")
@@ -95,6 +104,7 @@
     z, x = s // 4, s % 4
     up, down = c + 1, c - 1
     has_up, has_down = c < 63, c > 0
+    far_up, far_down = has_up & (c % 16 == 15), has_down & (c % 16 == 0)
 
     def partner(dz, dx):
         return ((z + dz) % 2) * 4 + (x + dx) % 4
@@ -203,10 +213,38 @@
         + jnp.where(slot < 1, 0.0, pltpu.roll(one, 1, 1))
         + jnp.where(slot < 2, 0.0, pltpu.roll(two, 2, 1))
     )
-    encoded = gelu(drawn)
     cell = cell_s[...]
     quality = quality_s[...]
     live = live_ref[0, 0]
+    packet = pltpu.make_async_remote_copy(
+        src_ref=pack_s,
+        dst_ref=packed_s,
+        send_sem=packet_sem.at[0],
+        recv_sem=packet_sem.at[1],
+        device_id=(s, down),
+        device_id_type=MESH,
+    )
+
+    @pl.when(far_down)
+    def _():
+        lane = lax.broadcasted_iota(jnp.int32, (64, 128), 1)
+        lane8 = lax.broadcasted_iota(jnp.int32, (8, 128), 1)
+        row8 = lax.broadcasted_iota(jnp.int32, (8, 128), 0)
+        pack_s[0:64] = jnp.where(
+            lane < 2, drawn[:, 0:128], pltpu.roll(asked_s[:, 0:128], 2, 1)
+        )
+        pack_s[64:72] = jnp.where(
+            row8 == 0,
+            quality[:, 0:128],
+            jnp.where(
+                row8 == 1,
+                cell[:, 0:128].astype(jnp.float32),
+                jnp.where(lane8 < live, 1.0, 0.0),
+            ),
+        )
+        packet.start()
+
+    encoded = gelu(drawn)
     score = jnp.sum(encoded * asked_s[...], axis=0, keepdims=True)
     score = score + quality
     valid = (slot < live) & (slot >= 2)
@@ -249,20 +287,65 @@
     sums = sums[0:64] * factor + query * prior_factor
     peak = joint
 
+    row = lax.broadcasted_iota(jnp.int32, (32, 256), 0)
+    chosen = lax.broadcasted_iota(jnp.int32, (32, 256), 1) == (
+        (row & 15) * 16 + jnp.where(row >= 16, 15, 0)
+    )
+    chosen = jnp.where(chosen, 1.0, 0.0)
+    chosen = jnp.concatenate([chosen] * 3, axis=1).astype(jnp.bfloat16)
+
+    def edge_rows(peak, total, sums):
+        rows = jnp.concatenate(
+            [sums, peak, total, jnp.zeros((62, 256), jnp.float32)], axis=0
+        )
+        rows = jnp.concatenate(split3(rows), axis=1).astype(jnp.bfloat16)
+        return dot(chosen, rows, turned, None)
+
+    def edge_copy(source, k, cell_to, target, out, into):
+        dz, dx = (OFFSETS + ((0, 0),))[k]
+        slot = dz * 4 + dx
+        return pltpu.make_async_remote_copy(
+            src_ref=source,
+            dst_ref=target.at[slot],
+            send_sem=out.at[slot],
+            recv_sem=into.at[slot],
+            device_id=(partner(dz, dx), cell_to),
+            device_id_type=MESH,
+        )
+
+    ups = [
+        edge_copy(edge_s.at[pl.ds(16, 16)], k, up, prev_s, up_out, up_in)
+        for k in range(8)
+    ]
+    downs, far_downs = (
+        [edge_copy(source, k, down, next_s, down_out, down_in) for k in range(8)]
+        for source in (edge_s.at[pl.ds(0, 16)], early_s)
+    )
+
+    @pl.when(far_down)
+    def _():
+        early_s[...] = edge_rows(peak, total, sums)[0:16]
+        pl.semaphore_wait(ready, 7)
+        for copy in far_downs:
+            copy.start()
+
     @pl.when(has_down)
     def _():
         tail.wait_recv()
 
     parity = (lax.broadcasted_iota(jnp.int32, (64, 128), 1) & 1) == 0
-    late = [
-        jnp.sum(enc_s[:, 0:128] * tail_s[t : t + 1], axis=1, keepdims=True)
-        + drawn[:, t : t + 1]
-        for t in range(2)
-    ]
-    late = gelu(jnp.where(parity, late[0], late[1]))
-    late_score = jnp.sum(
-        late * jnp.where(parity, asked_s[:, 0:1], asked_s[:, 1:2]), axis=0, keepdims=True
-    )
+
+    def late_tokens(rows, drawn, asked):
+        made = [
+            jnp.sum(enc_s[:, 0:128] * rows[t : t + 1], axis=1, keepdims=True)
+            + drawn[:, t : t + 1]
+            for t in range(2)
+        ]
+        made = gelu(jnp.where(parity, made[0], made[1]))
+        asked = jnp.where(parity, asked[:, 0:1], asked[:, 1:2])
+        return made, jnp.sum(made * asked, axis=0, keepdims=True)
+
+    late, late_score = late_tokens(tail_s[...], drawn[:, 0:128], asked_s[:, 0:2])
     cells = lax.broadcasted_iota(jnp.int32, (1, 256), 1)
     there = [(cells == cell[:, t : t + 1]) & (t < live) for t in range(2)]
     scores = [
@@ -299,40 +382,18 @@
             copy.start()
             parts.append(copy)
 
-    row = lax.broadcasted_iota(jnp.int32, (32, 256), 0)
-    chosen = lax.broadcasted_iota(jnp.int32, (32, 256), 1) == (
-        (row & 15) * 16 + jnp.where(row >= 16, 15, 0)
-    )
-    edge_s[...] = dot(
-        jnp.where(chosen, 1.0, 0.0),
-        jnp.concatenate([sums, span, jnp.zeros((62, 256), jnp.float32)], axis=0),
-        turned,
-    )
-    ups, downs = [], []
-    for dz, dx in OFFSETS + ((0, 0),):
-        slot = dz * 4 + dx
-        for rows, cell_to, target, out, into, kept in (
-            (16, up, prev_s, up_out, up_in, ups),
-            (0, down, next_s, down_out, down_in, downs),
-        ):
-            kept.append(
-                pltpu.make_async_remote_copy(
-                    src_ref=edge_s.at[pl.ds(rows, 16)],
-                    dst_ref=target.at[slot],
-                    send_sem=out.at[slot],
-                    recv_sem=into.at[slot],
-                    device_id=(partner(dz, dx), cell_to),
-                    device_id_type=MESH,
-                )
-            )
-    pl.semaphore_wait(ready, 7)
+    edge_s[...] = edge_rows(joint, total, sums)
+
+    @pl.when(jnp.logical_not(far_down))
+    def _():
+        pl.semaphore_wait(ready, 7)
 
     @pl.when(has_up)
     def _():
         for copy in ups:
             copy.start()
 
-    @pl.when(has_down)
+    @pl.when(has_down & jnp.logical_not(far_down))
     def _():
         for copy in downs:
             copy.start()
@@ -347,6 +408,48 @@
     near = near_s[...] - c * 256
     near_edge = ((near >> 4) & 15) + jnp.where(near < 0, 16, 0)
     near_side = (near < 0) | (near >= 256)
+
+    shared = []
+    for dz, dx in OFFSETS:
+        slot = dz * 4 + dx
+        shared.append(
+            pltpu.make_async_remote_copy(
+                src_ref=token_s,
+                dst_ref=tokens_s.at[slot],
+                send_sem=token_out.at[slot],
+                recv_sem=token_in.at[slot],
+                device_id=(partner(dz, dx), c),
+                device_id_type=MESH,
+            )
+        )
+
+    @pl.when(far_up)
+    def _():
+        packet.wait_recv()
+        made, made_score = late_tokens(
+            head_s[...], packed_s[0:64, 0:2], packed_s[0:64, 2:4]
+        )
+        made_score = jnp.where(
+            packed_s[66:67] > 0.0, made_score + packed_s[64:65], FLOOR
+        )
+        rows = jnp.transpose(made)[0:8]
+        row8 = lax.broadcasted_iota(jnp.int32, (8, 64), 0)
+        lane8 = lax.broadcasted_iota(jnp.int32, (8, 64), 1)
+        others = [
+            jnp.where(row8 == 0, one[:, 0:1], one[:, 1:2])
+            for one in (made_score, packed_s[65:66])
+        ]
+        token_s[...] = jnp.concatenate(
+            [
+                rows,
+                jnp.where(
+                    lane8 == 0, others[0], jnp.where(lane8 == 1, 1.0, others[1])
+                ),
+            ],
+            axis=1,
+        )
+        for copy in shared:
+            copy.start()
 
     own = send_s[s]
     for copy in parts:
@@ -384,13 +487,40 @@
         for copy in downs:
             copy.wait_recv()
 
-    edges = []
-    for side in (next_s, prev_s):
-        blocks = [side[k] for k in range(8)]
+    def mean(blocks):
         joint = functools.reduce(jnp.maximum, blocks)[:, 64:65]
         whole = sum(block * jnp.exp(block[:, 64:65] - joint) for block in blocks)
-        edges.append(whole[:, 0:64] / whole[:, 65:66])
-    edges = jnp.concatenate(edges + [jnp.zeros((96, 64), jnp.float32)], axis=0)
+        return whole[:, 0:64] / whole[:, 65:66]
+
+    below_blocks = [next_s[k] for k in range(8)]
+
+    @pl.when(jnp.logical_not(far_up))
+    def _():
+        side_s[...] = mean(below_blocks)
+
+    @pl.when(far_up)
+    def _():
+        for copy in shared:
+            copy.wait_recv()
+        first_cell = lax.broadcasted_iota(jnp.int32, (16, 128), 0).astype(jnp.float32) * 16.0
+        more = []
+        for tokens in [token_s[...]] + [tokens_s[k] for k in range(1, 8)]:
+            for t in range(2):
+                more.append(
+                    jnp.where(
+                        first_cell == tokens[t : t + 1, 66:67], tokens[t : t + 1], FLOOR
+                    )
+                )
+        side_s[...] = mean(below_blocks + more)
+
+    edges = jnp.concatenate(
+        [
+            side_s[...],
+            mean([prev_s[k] for k in range(8)]),
+            jnp.zeros((96, 64), jnp.float32),
+        ],
+        axis=0,
+    )
     outer = dot(stencil[8:72], edges, turned, HIGH)
 
     for copy in pools:
@@ -437,6 +567,15 @@
     @pl.when(has_down)
     def _():
         for copy in downs:
+            copy.wait_send()
+
+    @pl.when(far_down)
+    def _():
+        packet.wait_send()
+
+    @pl.when(far_up)
+    def _():
+        for copy in shared:
             copy.wait_send()
 
     for copy in parts + pools:
@@ -473,6 +612,12 @@
             pltpu.VMEM((8, 8, 256), f32),
             pltpu.VMEM((2, 256), f32),
             pltpu.VMEM((32, 128), f32),
+            pltpu.VMEM((16, 128), f32),
+            pltpu.VMEM((72, 128), f32),
+            pltpu.VMEM((72, 128), f32),
+            pltpu.VMEM((8, 128), f32),
+            pltpu.VMEM((8, 8, 128), f32),
+            pltpu.VMEM((16, 64), f32),
             pltpu.VMEM((8, 8, 256), f32),
             pltpu.VMEM((8, 2, 256), f32),
             pltpu.VMEM((8, 8, 256), f32),
@@ -482,7 +627,7 @@
             dma((2,)),
         ]
         + [dma((8,))] * 10
-        + [pltpu.SemaphoreType.REGULAR],
+        + [dma((2,)), dma((8,)), dma((8,)), pltpu.SemaphoreType.REGULAR],
         compiler_params=pltpu.CompilerParams(collective_id=0, has_side_effects=True),
     )(*operands)
 

time: 21.1 us -> 20.5 us (0.972)
  the two profiles are of different devices: /device:TPU:185 before, /device:TPU:256 now
where the time goes in v6:
time: 20.5 us; the launch traced here: 20.4 us
  Pallas kernels  19.1 us (93%)
  between operations  0.66 us (3%)
  local copies, waits for them, and re-layouts  0.6 us (3%)
    pallas_call x1, Pallas kernels, on_device(): pl.pallas_call(kernel, out_shape=pltpu.VMEM((8, 256), f32), in_specs=[pl....  19.1 us
    unnamed x1, local copies, waits for them, and re-layouts  0.6 us

profile of v6, /device:TPU:256, one launch (start us, length us, event | category | flops | bytes accessed | tf_op | source)
XLA Modules:
  0.0 20.4 jit_solution(5076609912820045649)
XLA Ops:
  0.7 19.1 %shard_map.100 = f32[8,256]{1,0:T(8,128)S(1)} custom-call(f32[1,64,512]{2,1,0:T(8,128)} %swath_ref.1, f32[1,64,192]{2,1,0:T(8,128)} %enc_ref.1, f32[64,64]{1,0:T(8,128)} %key_ref.1, f32[64,64]{1,0:T(8,128)} %value_ref.1, f32[64,256]{1,0:T(8,128)} %query_ref.1, f32[1,512]{1,0:T(1,128)} %quality_ref.1, s32[1,512]{1,0:T(1,128)} %cell_ref.1, ...), custom_call_target="tpu_custom_call" | custom-call | tf_op jit(solution)/shard_map/pallas_call | solution.py:588
  19.8 0.6 %copy.12 = f32[8,256]{1,0:T(8,128)} copy(f32[8,256]{1,0:T(8,128)S(1)} %shard_map.100) | data formatting | bytes 16384

commit v7 on v6

--- a/solution.py
+++ b/solution.py
@@ -62,7 +62,6 @@
     cell_s,
     near_s,
     hp_s,
-    mixed_s,
     hot_s,
     asked_s,
     prior_s,
@@ -76,6 +75,8 @@
     packed_s,
     token_s,
     tokens_s,
+    late_s,
+    lates_s,
     side_s,
     part_s,
     spans_s,
@@ -97,6 +98,8 @@
     packet_sem,
     token_out,
     token_in,
+    late_out,
+    late_in,
     ready,
 ):
     s = lax.axis_index("sensor")
@@ -141,8 +144,7 @@
         pl.semaphore_signal(
             barrier, inc=1, device_id=(partner(dz, dx), c), device_id_type=MESH
         )
-    for i in range(6):
-        loads[i].wait()
+    loads[0].wait()
     last = jnp.transpose(x_s[:, 384:512])
     row = lax.broadcasted_iota(jnp.int32, (8, 64), 0)
     head_s[...] = jnp.where(
@@ -157,6 +159,38 @@
         0.0,
     )
 
+    pl.semaphore_wait(
+        barrier, 7 + has_up.astype(jnp.int32) + has_down.astype(jnp.int32)
+    )
+    tail = pltpu.make_async_remote_copy(
+        src_ref=head_s,
+        dst_ref=tail_s,
+        send_sem=tail_sem.at[0],
+        recv_sem=tail_sem.at[1],
+        device_id=(s, up),
+        device_id_type=MESH,
+    )
+
+    @pl.when(has_up)
+    def _():
+        tail.start()
+
+    for dz, dx in OFFSETS:
+        pl.semaphore_signal(
+            ready, inc=1, device_id=(partner(dz, dx), c), device_id_type=MESH
+        )
+
+    @pl.when(jnp.logical_not(has_down))
+    def _():
+        tail_s[...] = jnp.zeros((8, 128), jnp.float32)
+        prev_s[...] = jnp.ones((8, 16, 128), jnp.float32)
+
+    @pl.when(jnp.logical_not(has_up))
+    def _():
+        next_s[...] = jnp.ones((8, 16, 128), jnp.float32)
+
+    for i in range(1, 6):
+        loads[i].wait()
     query = query_s[...]
     bilinear = full_dot(jnp.transpose(key_s[...]) * 0.125, query)
     cell = cell_s[...]
@@ -165,7 +199,7 @@
     ).astype(jnp.bfloat16)
     enc = enc_s[...]
     taps = jnp.concatenate([enc[:, 0:64], enc[:, 64:128], enc[:, 128:192]], axis=0)
-    mixed_s[...] = full_dot(taps, x_s[...])
+    mixed = full_dot(taps, x_s[...])
     for b in range(4):
         index = jnp.broadcast_to(cell[:, b * 128 : (b + 1) * 128], (64, 128))
         asked_s[:, b * 128 : (b + 1) * 128] = jnp.where(
@@ -175,37 +209,6 @@
         )
     prior_s[...] = jnp.sum(query * bilinear, axis=0, keepdims=True)
 
-    pl.semaphore_wait(
-        barrier, 7 + has_up.astype(jnp.int32) + has_down.astype(jnp.int32)
-    )
-    tail = pltpu.make_async_remote_copy(
-        src_ref=head_s,
-        dst_ref=tail_s,
-        send_sem=tail_sem.at[0],
-        recv_sem=tail_sem.at[1],
-        device_id=(s, up),
-        device_id_type=MESH,
-    )
-
-    @pl.when(has_up)
-    def _():
-        tail.start()
-
-    for dz, dx in OFFSETS:
-        pl.semaphore_signal(
-            ready, inc=1, device_id=(partner(dz, dx), c), device_id_type=MESH
-        )
-
-    @pl.when(jnp.logical_not(has_down))
-    def _():
-        tail_s[...] = jnp.zeros((8, 128), jnp.float32)
-        prev_s[...] = jnp.ones((8, 16, 128), jnp.float32)
-
-    @pl.when(jnp.logical_not(has_up))
-    def _():
-        next_s[...] = jnp.ones((8, 16, 128), jnp.float32)
-
-    mixed = mixed_s[...]
     two, one, zero = mixed[0:64], mixed[64:128], mixed[128:192]
     slot = lax.broadcasted_iota(jnp.int32, (1, 512), 1)
     drawn = (
@@ -322,8 +325,41 @@
         for source in (edge_s.at[pl.ds(0, 16)], early_s)
     )
 
+    parts, lates = [], []
+    for dz, dx in OFFSETS:
+        slot = dz * 4 + dx
+        to = partner(dz, dx)
+        for source, target, out, into in (
+            (send_s.at[to], part_s.at[slot], part_out, part_in),
+            (span_s, spans_s.at[slot], span_out, span_in),
+        ):
+            parts.append(
+                pltpu.make_async_remote_copy(
+                    src_ref=source,
+                    dst_ref=target,
+                    send_sem=out.at[slot],
+                    recv_sem=into.at[slot],
+                    device_id=(to, c),
+                    device_id_type=MESH,
+                )
+            )
+        lates.append(
+            pltpu.make_async_remote_copy(
+                src_ref=late_s.at[to],
+                dst_ref=lates_s.at[slot],
+                send_sem=late_out.at[slot],
+                recv_sem=late_in.at[slot],
+                device_id=(to, c),
+                device_id_type=MESH,
+            )
+        )
+
     @pl.when(far_down)
     def _():
+        span_s[...] = jnp.concatenate([peak, total], axis=0)
+        send_s[...] = sums.reshape(8, 8, 256)
+        for copy in parts:
+            copy.start()
         early_s[...] = edge_rows(peak, total, sums)[0:16]
         pl.semaphore_wait(ready, 7)
         for copy in far_downs:
@@ -346,6 +382,24 @@
         return made, jnp.sum(made * asked, axis=0, keepdims=True)
 
     late, late_score = late_tokens(tail_s[...], drawn[:, 0:128], asked_s[:, 0:2])
+
+    @pl.when(far_down)
+    def _():
+        lane = lax.broadcasted_iota(jnp.int32, (1, 128), 1)
+        where_t = (lane & 1) == 0
+        marks = [
+            jnp.where(where_t, one[:, 0:1], one[:, 1:2])
+            for one in (
+                jnp.where(lane < live, late_score + quality[:, 0:128], FLOOR),
+                cell[:, 0:128].astype(jnp.float32),
+            )
+        ]
+        late_s[...] = jnp.where(
+            lane < 64, late, jnp.where(lane < 96, marks[0], marks[1])
+        ).reshape(8, 8, 128)
+        for copy in lates:
+            copy.start()
+
     cells = lax.broadcasted_iota(jnp.int32, (1, 256), 1)
     there = [(cells == cell[:, t : t + 1]) & (t < live) for t in range(2)]
     scores = [
@@ -359,28 +413,12 @@
         weight = jnp.where(there[t], jnp.exp(scores[t] - joint), 0.0)
         total = total + weight
         sums = sums + late[:, t : t + 1] * weight
-    span = jnp.concatenate([joint, total], axis=0)
-    span_s[...] = span
-    send_s[...] = sums.reshape(8, 8, 256)
-
-    parts = []
-    for dz, dx in OFFSETS:
-        slot = dz * 4 + dx
-        to = partner(dz, dx)
-        for source, target, out, into in (
-            (send_s.at[to], part_s.at[slot], part_out, part_in),
-            (span_s, spans_s.at[slot], span_out, span_in),
-        ):
-            copy = pltpu.make_async_remote_copy(
-                src_ref=source,
-                dst_ref=target,
-                send_sem=out.at[slot],
-                recv_sem=into.at[slot],
-                device_id=(to, c),
-                device_id_type=MESH,
-            )
+    @pl.when(jnp.logical_not(far_down))
+    def _():
+        span_s[...] = jnp.concatenate([joint, total], axis=0)
+        send_s[...] = sums.reshape(8, 8, 256)
+        for copy in parts:
             copy.start()
-            parts.append(copy)
 
     edge_s[...] = edge_rows(joint, total, sums)
 
@@ -451,17 +489,44 @@
         for copy in shared:
             copy.start()
 
-    own = send_s[s]
     for copy in parts:
         copy.wait_recv()
-    blocks = [own] + [part_s[k] for k in range(1, 8)]
-    spans = [span] + [spans_s[k] for k in range(1, 8)]
+    blocks = [send_s[s]] + [part_s[k] for k in range(1, 8)]
+    spans = [span_s[...]] + [spans_s[k] for k in range(1, 8)]
     peaks = jnp.concatenate([one[0:1] for one in spans], axis=0)
     totals = jnp.concatenate([one[1:2] for one in spans], axis=0)
-    factor = jnp.exp(peaks - jnp.max(peaks, axis=0, keepdims=True))
-    below = jnp.sum(totals * factor, axis=0, keepdims=True)
-    above = sum(blocks[k] * factor[k : k + 1] for k in range(8))
-    pool_s[s] = above / below
+    joint = jnp.max(peaks, axis=0, keepdims=True)
+
+    @pl.when(jnp.logical_not(far_down))
+    def _():
+        factor = jnp.exp(peaks - joint)
+        below = jnp.sum(totals * factor, axis=0, keepdims=True)
+        pool_s[s] = sum(blocks[k] * factor[k : k + 1] for k in range(8)) / below
+
+    @pl.when(far_down)
+    def _():
+        for copy in lates:
+            copy.wait_recv()
+        cells = lax.broadcasted_iota(jnp.int32, (8, 256), 1).astype(jnp.float32)
+        tiles = [late_s[s]] + [lates_s[k] for k in range(1, 8)]
+        entries = []
+        for t in range(2):
+            scores = jnp.concatenate([one[0:1, 64 + t : 65 + t] for one in tiles], axis=0)
+            places = jnp.concatenate([one[0:1, 96 + t : 97 + t] for one in tiles], axis=0)
+            entries.append(jnp.where(cells == places, scores, FLOOR))
+        all_joint = jnp.maximum(
+            joint, jnp.max(jnp.maximum(entries[0], entries[1]), axis=0, keepdims=True)
+        )
+        factor = jnp.exp(peaks - all_joint)
+        below = jnp.sum(totals * factor, axis=0, keepdims=True)
+        above = sum(blocks[k] * factor[k : k + 1] for k in range(8))
+        for t in range(2):
+            weight = jnp.exp(entries[t] - all_joint)
+            below = below + jnp.sum(weight, axis=0, keepdims=True)
+            above = above + sum(
+                tiles[k][:, t : t + 1] * weight[k : k + 1] for k in range(8)
+            )
+        pool_s[s] = above / below
 
     pools = []
     for dz, dx in OFFSETS:
@@ -571,7 +636,8 @@
 
     @pl.when(far_down)
     def _():
-        packet.wait_send()
+        for copy in [packet] + lates:
+            copy.wait_send()
 
     @pl.when(far_up)
     def _():
@@ -603,7 +669,6 @@
             pltpu.VMEM((1, 512), i32),
             pltpu.VMEM((8, 256), i32),
             pltpu.VMEM((8, 576), f32),
-            pltpu.VMEM((192, 512), f32),
             pltpu.VMEM((256, 512), jnp.bfloat16),
             pltpu.VMEM((64, 512), f32),
             pltpu.VMEM((1, 256), f32),
@@ -617,6 +682,8 @@
             pltpu.VMEM((72, 128), f32),
             pltpu.VMEM((8, 128), f32),
             pltpu.VMEM((8, 8, 128), f32),
+            pltpu.VMEM((8, 8, 128), f32),
+            pltpu.VMEM((8, 8, 128), f32),
             pltpu.VMEM((16, 64), f32),
             pltpu.VMEM((8, 8, 256), f32),
             pltpu.VMEM((8, 2, 256), f32),
@@ -627,7 +694,9 @@
             dma((2,)),
         ]
         + [dma((8,))] * 10
-        + [dma((2,)), dma((8,)), dma((8,)), pltpu.SemaphoreType.REGULAR],
+        + [dma((2,))]
+        + [dma((8,))] * 4
+        + [pltpu.SemaphoreType.REGULAR],
         compiler_params=pltpu.CompilerParams(collective_id=0, has_side_effects=True),
     )(*operands)
 

time: 20.5 us -> 20.2 us (0.985)
  Pallas kernels: 19.1 us -> 18.8 us
    pallas_call x1, Pallas kernels: 19.1 us -> 18.8 us  [on_device(): pl.pallas_call(kernel, out_shape=pltpu.VMEM((8, 256), f32), in_specs=[pl....]
where the time goes in v7:
time: 20.2 us; the launch traced here: 20 us
  Pallas kernels  18.8 us (93%)
  between operations  0.66 us (3%)
  local copies, waits for them, and re-layouts  0.6 us (3%)
    pallas_call x1, Pallas kernels, on_device(): pl.pallas_call(kernel, out_shape=pltpu.VMEM((8, 256), f32), in_specs=[pl....  18.8 us
    unnamed x1, local copies, waits for them, and re-layouts  0.6 us

profile of v7, /device:TPU:256, one launch (start us, length us, event | category | flops | bytes accessed | tf_op | source)
XLA Modules:
  0.0 20.0 jit_solution(13409979895866446153)
XLA Ops:
  0.7 18.8 %shard_map.100 = f32[8,256]{1,0:T(8,128)S(1)} custom-call(f32[1,64,512]{2,1,0:T(8,128)} %swath_ref.1, f32[1,64,192]{2,1,0:T(8,128)} %enc_ref.1, f32[64,64]{1,0:T(8,128)} %key_ref.1, f32[64,64]{1,0:T(8,128)} %value_ref.1, f32[64,256]{1,0:T(8,128)} %query_ref.1, f32[1,512]{1,0:T(1,128)} %quality_ref.1, s32[1,512]{1,0:T(1,128)} %cell_ref.1, ...), custom_call_target="tpu_custom_call" | custom-call | tf_op jit(solution)/shard_map/pallas_call | solution.py:654
  19.4 0.6 %copy.12 = f32[8,256]{1,0:T(8,128)} copy(f32[8,256]{1,0:T(8,128)S(1)} %shard_map.100) | data formatting | bytes 16384

commit v8 on v7

--- a/solution.py
+++ b/solution.py
@@ -75,8 +75,7 @@
     packed_s,
     token_s,
     tokens_s,
-    late_s,
-    lates_s,
+    pooled_s,
     side_s,
     part_s,
     spans_s,
@@ -98,8 +97,6 @@
     packet_sem,
     token_out,
     token_in,
-    late_out,
-    late_in,
     ready,
 ):
     s = lax.axis_index("sensor")
@@ -108,6 +105,7 @@
     up, down = c + 1, c - 1
     has_up, has_down = c < 63, c > 0
     far_up, far_down = has_up & (c % 16 == 15), has_down & (c % 16 == 0)
+    ahead = c % 16 == 0
 
     def partner(dz, dx):
         return ((z + dz) % 2) * 4 + (x + dx) % 4
@@ -211,10 +209,15 @@
 
     two, one, zero = mixed[0:64], mixed[64:128], mixed[128:192]
     slot = lax.broadcasted_iota(jnp.int32, (1, 512), 1)
-    drawn = (
-        zero
-        + jnp.where(slot < 1, 0.0, pltpu.roll(one, 1, 1))
-        + jnp.where(slot < 2, 0.0, pltpu.roll(two, 2, 1))
+    one, two = pltpu.roll(one, 1, 1), pltpu.roll(two, 2, 1)
+    begin = slot[:, 0:128]
+    drawn = zero + jnp.concatenate(
+        [
+            jnp.where(begin < 1, 0.0, one[:, 0:128])
+            + jnp.where(begin < 2, 0.0, two[:, 0:128]),
+            one[:, 128:] + two[:, 128:],
+        ],
+        axis=1,
     )
     cell = cell_s[...]
     quality = quality_s[...]
@@ -250,7 +253,7 @@
     encoded = gelu(drawn)
     score = jnp.sum(encoded * asked_s[...], axis=0, keepdims=True)
     score = score + quality
-    valid = (slot < live) & (slot >= 2)
+    valid = (slot < live) & (slot >= jnp.where(has_down, 2, 0))
 
     hot = lax.broadcasted_iota(jnp.int32, (256, 512), 0) == cell
     masked = jnp.where(valid, score, FLOOR)
@@ -325,7 +328,7 @@
         for source in (edge_s.at[pl.ds(0, 16)], early_s)
     )
 
-    parts, lates = [], []
+    parts = []
     for dz, dx in OFFSETS:
         slot = dz * 4 + dx
         to = partner(dz, dx)
@@ -343,109 +346,6 @@
                     device_id_type=MESH,
                 )
             )
-        lates.append(
-            pltpu.make_async_remote_copy(
-                src_ref=late_s.at[to],
-                dst_ref=lates_s.at[slot],
-                send_sem=late_out.at[slot],
-                recv_sem=late_in.at[slot],
-                device_id=(to, c),
-                device_id_type=MESH,
-            )
-        )
-
-    @pl.when(far_down)
-    def _():
-        span_s[...] = jnp.concatenate([peak, total], axis=0)
-        send_s[...] = sums.reshape(8, 8, 256)
-        for copy in parts:
-            copy.start()
-        early_s[...] = edge_rows(peak, total, sums)[0:16]
-        pl.semaphore_wait(ready, 7)
-        for copy in far_downs:
-            copy.start()
-
-    @pl.when(has_down)
-    def _():
-        tail.wait_recv()
-
-    parity = (lax.broadcasted_iota(jnp.int32, (64, 128), 1) & 1) == 0
-
-    def late_tokens(rows, drawn, asked):
-        made = [
-            jnp.sum(enc_s[:, 0:128] * rows[t : t + 1], axis=1, keepdims=True)
-            + drawn[:, t : t + 1]
-            for t in range(2)
-        ]
-        made = gelu(jnp.where(parity, made[0], made[1]))
-        asked = jnp.where(parity, asked[:, 0:1], asked[:, 1:2])
-        return made, jnp.sum(made * asked, axis=0, keepdims=True)
-
-    late, late_score = late_tokens(tail_s[...], drawn[:, 0:128], asked_s[:, 0:2])
-
-    @pl.when(far_down)
-    def _():
-        lane = lax.broadcasted_iota(jnp.int32, (1, 128), 1)
-        where_t = (lane & 1) == 0
-        marks = [
-            jnp.where(where_t, one[:, 0:1], one[:, 1:2])
-            for one in (
-                jnp.where(lane < live, late_score + quality[:, 0:128], FLOOR),
-                cell[:, 0:128].astype(jnp.float32),
-            )
-        ]
-        late_s[...] = jnp.where(
-            lane < 64, late, jnp.where(lane < 96, marks[0], marks[1])
-        ).reshape(8, 8, 128)
-        for copy in lates:
-            copy.start()
-
-    cells = lax.broadcasted_iota(jnp.int32, (1, 256), 1)
-    there = [(cells == cell[:, t : t + 1]) & (t < live) for t in range(2)]
-    scores = [
-        jnp.where(there[t], late_score[:, t : t + 1] + quality[:, t : t + 1], FLOOR)
-        for t in range(2)
-    ]
-    joint = jnp.maximum(peak, jnp.maximum(scores[0], scores[1]))
-    factor = jnp.exp(peak - joint)
-    total, sums = total * factor, sums * factor
-    for t in range(2):
-        weight = jnp.where(there[t], jnp.exp(scores[t] - joint), 0.0)
-        total = total + weight
-        sums = sums + late[:, t : t + 1] * weight
-    @pl.when(jnp.logical_not(far_down))
-    def _():
-        span_s[...] = jnp.concatenate([joint, total], axis=0)
-        send_s[...] = sums.reshape(8, 8, 256)
-        for copy in parts:
-            copy.start()
-
-    edge_s[...] = edge_rows(joint, total, sums)
-
-    @pl.when(jnp.logical_not(far_down))
-    def _():
-        pl.semaphore_wait(ready, 7)
-
-    @pl.when(has_up)
-    def _():
-        for copy in ups:
-            copy.start()
-
-    @pl.when(has_down & jnp.logical_not(far_down))
-    def _():
-        for copy in downs:
-            copy.start()
-
-    for i in range(6, 9):
-        loads[i].wait()
-    hp = hp_s[...]
-    stacked = jnp.concatenate([hp[:, k * 64 : (k + 1) * 64] for k in range(9)], axis=0)
-    stencil = dot(stacked, value_s[...])
-    part0, part1, _ = split3(stencil)
-    stencil_parts = jnp.concatenate([part0, part1, part0], axis=1).astype(jnp.bfloat16)
-    near = near_s[...] - c * 256
-    near_edge = ((near >> 4) & 15) + jnp.where(near < 0, 16, 0)
-    near_side = (near < 0) | (near >= 256)
 
     shared = []
     for dz, dx in OFFSETS:
@@ -461,33 +361,123 @@
             )
         )
 
+    def share(made, made_score, cells):
+        row = lax.broadcasted_iota(jnp.int32, (8, 64), 0)
+        column = lax.broadcasted_iota(jnp.int32, (8, 64), 1)
+        marks = [
+            jnp.where(row == 0, one[:, 0:1], one[:, 1:2]) for one in (made_score, cells)
+        ]
+        token_s[...] = jnp.concatenate(
+            [
+                jnp.transpose(made)[0:8],
+                jnp.where(column == 0, marks[0], jnp.where(column == 1, 1.0, marks[1])),
+            ],
+            axis=1,
+        )
+        for copy in shared:
+            copy.start()
+
+    @pl.when(ahead)
+    def _():
+        span_s[...] = jnp.concatenate([peak, total], axis=0)
+        send_s[...] = sums.reshape(8, 8, 256)
+        for copy in parts:
+            copy.start()
+
+    @pl.when(far_down)
+    def _():
+        early_s[...] = edge_rows(peak, total, sums)[0:16]
+        pl.semaphore_wait(ready, 7)
+        for copy in far_downs:
+            copy.start()
+
+    @pl.when(has_down)
+    def _():
+        tail.wait_recv()
+
+    parity = (lax.broadcasted_iota(jnp.int32, (64, 128), 1) & 1) == 0
+
+    def late_tokens(rows, drawn, asked):
+        made = [
+            jnp.sum(enc_s[:, 0:128] * rows[t : t + 1], axis=1, keepdims=True)
+            + drawn[:, t : t + 1]
+            for t in range(2)
+        ]
+        made = gelu(jnp.where(parity, made[0], made[1]))
+        asked = jnp.where(parity, asked[:, 0:1], asked[:, 1:2])
+        return made, jnp.sum(made * asked, axis=0, keepdims=True)
+
+    late, late_score = late_tokens(tail_s[...], drawn[:, 0:128], asked_s[:, 0:2])
+
+    @pl.when(far_down)
+    def _():
+        column = lax.broadcasted_iota(jnp.int32, (1, 128), 1)
+        share(
+            late,
+            jnp.where(column < live, late_score + quality[:, 0:128], FLOOR),
+            cell[:, 0:128].astype(jnp.float32),
+        )
+
+    cells = lax.broadcasted_iota(jnp.int32, (1, 256), 1)
+    there = [
+        (cells == cell[:, t : t + 1]) & (t < live) & has_down for t in range(2)
+    ]
+    scores = [
+        jnp.where(there[t], late_score[:, t : t + 1] + quality[:, t : t + 1], FLOOR)
+        for t in range(2)
+    ]
+    joint = jnp.maximum(peak, jnp.maximum(scores[0], scores[1]))
+    factor = jnp.exp(peak - joint)
+    total, sums = total * factor, sums * factor
+    for t in range(2):
+        weight = jnp.where(there[t], jnp.exp(scores[t] - joint), 0.0)
+        total = total + weight
+        sums = sums + late[:, t : t + 1] * weight
+    @pl.when(jnp.logical_not(ahead))
+    def _():
+        span_s[...] = jnp.concatenate([joint, total], axis=0)
+        send_s[...] = sums.reshape(8, 8, 256)
+        for copy in parts:
+            copy.start()
+
+    edge_s[...] = edge_rows(joint, total, sums)
+
+    @pl.when(jnp.logical_not(far_down))
+    def _():
+        pl.semaphore_wait(ready, 7)
+
+    @pl.when(has_up)
+    def _():
+        for copy in ups:
+            copy.start()
+
+    @pl.when(has_down & jnp.logical_not(far_down))
+    def _():
+        for copy in downs:
+            copy.start()
+
+    for i in range(6, 9):
+        loads[i].wait()
+    hp = hp_s[...]
+    stacked = jnp.concatenate([hp[:, k * 64 : (k + 1) * 64] for k in range(9)], axis=0)
+    stencil = dot(stacked, value_s[...])
+    part0, part1, _ = split3(stencil)
+    stencil_parts = jnp.concatenate([part0, part1, part0], axis=1).astype(jnp.bfloat16)
+    near = near_s[...] - c * 256
+    near_edge = ((near >> 4) & 15) + jnp.where(near < 0, 16, 0)
+    near_side = (near < 0) | (near >= 256)
+
     @pl.when(far_up)
     def _():
         packet.wait_recv()
         made, made_score = late_tokens(
             head_s[...], packed_s[0:64, 0:2], packed_s[0:64, 2:4]
         )
-        made_score = jnp.where(
-            packed_s[66:67] > 0.0, made_score + packed_s[64:65], FLOOR
-        )
-        rows = jnp.transpose(made)[0:8]
-        row8 = lax.broadcasted_iota(jnp.int32, (8, 64), 0)
-        lane8 = lax.broadcasted_iota(jnp.int32, (8, 64), 1)
-        others = [
-            jnp.where(row8 == 0, one[:, 0:1], one[:, 1:2])
-            for one in (made_score, packed_s[65:66])
-        ]
-        token_s[...] = jnp.concatenate(
-            [
-                rows,
-                jnp.where(
-                    lane8 == 0, others[0], jnp.where(lane8 == 1, 1.0, others[1])
-                ),
-            ],
-            axis=1,
-        )
-        for copy in shared:
-            copy.start()
+        share(
+            made,
+            jnp.where(packed_s[66:67] > 0.0, made_score + packed_s[64:65], FLOOR),
+            packed_s[65:66],
+        )
 
     for copy in parts:
         copy.wait_recv()
@@ -496,37 +486,9 @@
     peaks = jnp.concatenate([one[0:1] for one in spans], axis=0)
     totals = jnp.concatenate([one[1:2] for one in spans], axis=0)
     joint = jnp.max(peaks, axis=0, keepdims=True)
-
-    @pl.when(jnp.logical_not(far_down))
-    def _():
-        factor = jnp.exp(peaks - joint)
-        below = jnp.sum(totals * factor, axis=0, keepdims=True)
-        pool_s[s] = sum(blocks[k] * factor[k : k + 1] for k in range(8)) / below
-
-    @pl.when(far_down)
-    def _():
-        for copy in lates:
-            copy.wait_recv()
-        cells = lax.broadcasted_iota(jnp.int32, (8, 256), 1).astype(jnp.float32)
-        tiles = [late_s[s]] + [lates_s[k] for k in range(1, 8)]
-        entries = []
-        for t in range(2):
-            scores = jnp.concatenate([one[0:1, 64 + t : 65 + t] for one in tiles], axis=0)
-            places = jnp.concatenate([one[0:1, 96 + t : 97 + t] for one in tiles], axis=0)
-            entries.append(jnp.where(cells == places, scores, FLOOR))
-        all_joint = jnp.maximum(
-            joint, jnp.max(jnp.maximum(entries[0], entries[1]), axis=0, keepdims=True)
-        )
-        factor = jnp.exp(peaks - all_joint)
-        below = jnp.sum(totals * factor, axis=0, keepdims=True)
-        above = sum(blocks[k] * factor[k : k + 1] for k in range(8))
-        for t in range(2):
-            weight = jnp.exp(entries[t] - all_joint)
-            below = below + jnp.sum(weight, axis=0, keepdims=True)
-            above = above + sum(
-                tiles[k][:, t : t + 1] * weight[k : k + 1] for k in range(8)
-            )
-        pool_s[s] = above / below
+    factor = jnp.exp(peaks - joint)
+    below = jnp.sum(totals * factor, axis=0, keepdims=True)
+    pool_s[s] = sum(blocks[k] * factor[k : k + 1] for k in range(8)) / below
 
     pools = []
     for dz, dx in OFFSETS:
@@ -587,42 +549,61 @@
         axis=0,
     )
     outer = dot(stencil[8:72], edges, turned, HIGH)
+    outside = []
+    for h in range(2):
+        cut = slice(h * 128, (h + 1) * 128)
+        part = jnp.zeros((8, 128), jnp.float32)
+        for k in range(8):
+            index = jnp.broadcast_to(near_edge[k : k + 1, cut], (8, 128))
+            side = jnp.broadcast_to(near_side[k : k + 1, cut], (8, 128))
+            part = part + jnp.where(
+                side, lanes(outer[k * 8 : (k + 1) * 8], index), 0.0
+            )
+        outside.append(part)
 
     for copy in pools:
         copy.wait_recv()
-    part0, part1, _ = split3(pool_s[...].reshape(64, 256))
+
+    @pl.when(jnp.logical_not(far_down))
+    def _():
+        pooled_s[...] = pool_s[...].reshape(64, 256)
+
+    @pl.when(far_down)
+    def _():
+        for copy in shared:
+            copy.wait_recv()
+        rows = jnp.concatenate(
+            [token_s[0:2]] + [tokens_s[k, 0:2] for k in range(1, 8)], axis=0
+        )
+        cells = lax.broadcasted_iota(jnp.int32, (16, 256), 1).astype(jnp.float32)
+        entries = jnp.where(cells == rows[:, 66:67], rows[:, 64:65], FLOOR)
+        all_joint = jnp.maximum(joint, jnp.max(entries, axis=0, keepdims=True))
+        weight = jnp.exp(entries - all_joint)
+        old = below * jnp.exp(joint - all_joint)
+        pooled_s[...] = (
+            pool_s[...].reshape(64, 256) * old + dot(rows[:, 0:64], weight, ((0,), (0,)))
+        ) / (old + jnp.sum(weight, axis=0, keepdims=True))
+
+    part0, part1, _ = split3(pooled_s[...])
     inner = dot(
         stencil_parts,
         jnp.concatenate([part0, part0, part1], axis=0).astype(jnp.bfloat16),
         precision=None,
     )
-    joined = inner[0:8]
-    picked = []
-    for k in range(8):
-        index = jnp.broadcast_to(near[k : k + 1], (8, 256))
-        row = inner[8 + k * 8 : 16 + k * 8]
-        halves = []
-        for h in range(2):
-            part = index[:, h * 128 : (h + 1) * 128]
-            halves.append(
-                jnp.where(
-                    (part & 128) > 0,
-                    lanes(row[:, 128:], part & 127),
-                    lanes(row[:, :128], part & 127),
-                )
+    for h in range(2):
+        cut = slice(h * 128, (h + 1) * 128)
+        joined = inner[0:8, cut] + outside[h]
+        for k in range(8):
+            row = inner[8 + k * 8 : 16 + k * 8]
+            index = jnp.broadcast_to(near[k : k + 1, cut], (8, 128))
+            side = jnp.broadcast_to(near_side[k : k + 1, cut], (8, 128))
+            picked = jnp.where(
+                (index & 128) > 0,
+                lanes(row[:, 128:], index & 127),
+                lanes(row[:, :128], index & 127),
             )
-        picked.append(halves)
-
-    for h in range(2):
-        total = joined[:, h * 128 : (h + 1) * 128]
-        for k in range(8):
-            cut = slice(h * 128, (h + 1) * 128)
-            index = jnp.broadcast_to(near_edge[k : k + 1, cut], (8, 128))
-            side = jnp.broadcast_to(near_side[k : k + 1, cut], (8, 128))
-            total = total + jnp.where(
-                side, lanes(outer[k * 8 : (k + 1) * 8], index), picked[k][h]
-            )
-        out_ref[:, h * 128 : (h + 1) * 128] = total
+            joined = joined + jnp.where(side, 0.0, picked)
+        out_ref[:, cut] = joined
 
     @pl.when(has_up)
     def _():
@@ -636,10 +617,9 @@
 
     @pl.when(far_down)
     def _():
-        for copy in [packet] + lates:
-            copy.wait_send()
-
-    @pl.when(far_up)
+        packet.wait_send()
+
+    @pl.when(far_up | far_down)
     def _():
         for copy in shared:
             copy.wait_send()
@@ -682,8 +662,7 @@
             pltpu.VMEM((72, 128), f32),
             pltpu.VMEM((8, 128), f32),
             pltpu.VMEM((8, 8, 128), f32),
-            pltpu.VMEM((8, 8, 128), f32),
-            pltpu.VMEM((8, 8, 128), f32),
+            pltpu.VMEM((64, 256), f32),
             pltpu.VMEM((16, 64), f32),
             pltpu.VMEM((8, 8, 256), f32),
             pltpu.VMEM((8, 2, 256), f32),
@@ -695,7 +674,7 @@
         ]
         + [dma((8,))] * 10
         + [dma((2,))]
-        + [dma((8,))] * 4
+        + [dma((8,))] * 2
         + [pltpu.SemaphoreType.REGULAR],
         compiler_params=pltpu.CompilerParams(collective_id=0, has_side_effects=True),
     )(*operands)

time: 20.2 us -> 19.6 us (0.970)
  the two profiles are of different devices: /device:TPU:256 before, /device:TPU:1 now
where the time goes in v8:
time: 19.6 us; the launch traced here: 19.4 us
  Pallas kernels  18.2 us (93%)
  between operations  0.66 us (3%)
  local copies, waits for them, and re-layouts  0.6 us (3%)
    pallas_call x1, Pallas kernels, on_device(): pl.pallas_call(kernel, out_shape=pltpu.VMEM((8, 256), f32), in_specs=[pl....  18.2 us
    unnamed x1, local copies, waits for them, and re-layouts  0.6 us

profile of v8, /device:TPU:1, one launch (start us, length us, event | category | flops | bytes accessed | tf_op | source)
XLA Modules:
  0.0 19.4 jit_solution(6345190048655620515)
XLA Ops:
  0.7 18.2 %shard_map.100 = f32[8,256]{1,0:T(8,128)S(1)} custom-call(f32[1,64,512]{2,1,0:T(8,128)} %swath_ref.1, f32[1,64,192]{2,1,0:T(8,128)} %enc_ref.1, f32[64,64]{1,0:T(8,128)} %key_ref.1, f32[64,64]{1,0:T(8,128)} %value_ref.1, f32[64,256]{1,0:T(8,128)} %query_ref.1, f32[1,512]{1,0:T(1,128)} %quality_ref.1, s32[1,512]{1,0:T(1,128)} %cell_ref.1, ...), custom_call_target="tpu_custom_call" | custom-call | tf_op jit(solution)/shard_map/pallas_call | solution.py:634
  18.8 0.6 %copy.12 = f32[8,256]{1,0:T(8,128)} copy(f32[8,256]{1,0:T(8,128)S(1)} %shard_map.100) | data formatting | bytes 16384

commit v9 on v8

--- a/solution.py
+++ b/solution.py
@@ -75,7 +75,10 @@
     packed_s,
     token_s,
     tokens_s,
-    pooled_s,
+    far_s,
+    fars_s,
+    scale_s,
+    shift_s,
     side_s,
     part_s,
     spans_s,
@@ -97,6 +100,8 @@
     packet_sem,
     token_out,
     token_in,
+    far_out,
+    far_in,
     ready,
 ):
     s = lax.axis_index("sensor")
@@ -105,7 +110,6 @@
     up, down = c + 1, c - 1
     has_up, has_down = c < 63, c > 0
     far_up, far_down = has_up & (c % 16 == 15), has_down & (c % 16 == 0)
-    ahead = c % 16 == 0
 
     def partner(dz, dx):
         return ((z + dz) % 2) * 4 + (x + dx) % 4
@@ -142,7 +146,8 @@
         pl.semaphore_signal(
             barrier, inc=1, device_id=(partner(dz, dx), c), device_id_type=MESH
         )
-    loads[0].wait()
+    for i in range(6):
+        loads[i].wait()
     last = jnp.transpose(x_s[:, 384:512])
     row = lax.broadcasted_iota(jnp.int32, (8, 64), 0)
     head_s[...] = jnp.where(
@@ -157,38 +162,6 @@
         0.0,
     )
 
-    pl.semaphore_wait(
-        barrier, 7 + has_up.astype(jnp.int32) + has_down.astype(jnp.int32)
-    )
-    tail = pltpu.make_async_remote_copy(
-        src_ref=head_s,
-        dst_ref=tail_s,
-        send_sem=tail_sem.at[0],
-        recv_sem=tail_sem.at[1],
-        device_id=(s, up),
-        device_id_type=MESH,
-    )
-
-    @pl.when(has_up)
-    def _():
-        tail.start()
-
-    for dz, dx in OFFSETS:
-        pl.semaphore_signal(
-            ready, inc=1, device_id=(partner(dz, dx), c), device_id_type=MESH
-        )
-
-    @pl.when(jnp.logical_not(has_down))
-    def _():
-        tail_s[...] = jnp.zeros((8, 128), jnp.float32)
-        prev_s[...] = jnp.ones((8, 16, 128), jnp.float32)
-
-    @pl.when(jnp.logical_not(has_up))
-    def _():
-        next_s[...] = jnp.ones((8, 16, 128), jnp.float32)
-
-    for i in range(1, 6):
-        loads[i].wait()
     query = query_s[...]
     bilinear = full_dot(jnp.transpose(key_s[...]) * 0.125, query)
     cell = cell_s[...]
@@ -219,6 +192,37 @@
         ],
         axis=1,
     )
+
+    pl.semaphore_wait(
+        barrier, 7 + has_up.astype(jnp.int32) + has_down.astype(jnp.int32)
+    )
+    tail = pltpu.make_async_remote_copy(
+        src_ref=head_s,
+        dst_ref=tail_s,
+        send_sem=tail_sem.at[0],
+        recv_sem=tail_sem.at[1],
+        device_id=(s, up),
+        device_id_type=MESH,
+    )
+
+    @pl.when(has_up)
+    def _():
+        tail.start()
+
+    for dz, dx in OFFSETS:
+        pl.semaphore_signal(
+            ready, inc=1, device_id=(partner(dz, dx), c), device_id_type=MESH
+        )
+
+    @pl.when(jnp.logical_not(has_down))
+    def _():
+        tail_s[...] = jnp.zeros((8, 128), jnp.float32)
+        prev_s[...] = jnp.ones((8, 16, 128), jnp.float32)
+
+    @pl.when(jnp.logical_not(has_up))
+    def _():
+        next_s[...] = jnp.ones((8, 16, 128), jnp.float32)
+
     cell = cell_s[...]
     quality = quality_s[...]
     live = live_ref[0, 0]
@@ -347,42 +351,44 @@
                 )
             )
 
-    shared = []
-    for dz, dx in OFFSETS:
-        slot = dz * 4 + dx
-        shared.append(
+    shared, far_shared = (
+        [
             pltpu.make_async_remote_copy(
-                src_ref=token_s,
-                dst_ref=tokens_s.at[slot],
-                send_sem=token_out.at[slot],
-                recv_sem=token_in.at[slot],
+                src_ref=source,
+                dst_ref=target.at[dz * 4 + dx],
+                send_sem=out.at[dz * 4 + dx],
+                recv_sem=into.at[dz * 4 + dx],
                 device_id=(partner(dz, dx), c),
                 device_id_type=MESH,
             )
-        )
-
-    def share(made, made_score, cells):
+            for dz, dx in OFFSETS
+        ]
+        for source, target, out, into in (
+            (token_s, tokens_s, token_out, token_in),
+            (far_s, fars_s, far_out, far_in),
+        )
+    )
+
+    def share(target, copies, made, made_score, cells):
         row = lax.broadcasted_iota(jnp.int32, (8, 64), 0)
         column = lax.broadcasted_iota(jnp.int32, (8, 64), 1)
         marks = [
             jnp.where(row == 0, one[:, 0:1], one[:, 1:2]) for one in (made_score, cells)
         ]
-        token_s[...] = jnp.concatenate(
+        target[...] = jnp.concatenate(
             [
                 jnp.transpose(made)[0:8],
                 jnp.where(column == 0, marks[0], jnp.where(column == 1, 1.0, marks[1])),
             ],
             axis=1,
         )
-        for copy in shared:
+        for copy in copies:
             copy.start()
 
-    @pl.when(ahead)
-    def _():
-        span_s[...] = jnp.concatenate([peak, total], axis=0)
-        send_s[...] = sums.reshape(8, 8, 256)
-        for copy in parts:
-            copy.start()
+    span_s[...] = jnp.concatenate([peak, total], axis=0)
+    send_s[...] = sums.reshape(8, 8, 256)
+    for copy in parts:
+        copy.start()
 
     @pl.when(far_down)
     def _():
@@ -409,15 +415,17 @@
 
     late, late_score = late_tokens(tail_s[...], drawn[:, 0:128], asked_s[:, 0:2])
 
-    @pl.when(far_down)
-    def _():
+    def share_own():
         column = lax.broadcasted_iota(jnp.int32, (1, 128), 1)
         share(
+            token_s,
+            shared,
             late,
             jnp.where(column < live, late_score + quality[:, 0:128], FLOOR),
             cell[:, 0:128].astype(jnp.float32),
         )
 
+    pl.when(far_down)(share_own)
     cells = lax.broadcasted_iota(jnp.int32, (1, 256), 1)
     there = [
         (cells == cell[:, t : t + 1]) & (t < live) & has_down for t in range(2)
@@ -433,12 +441,6 @@
         weight = jnp.where(there[t], jnp.exp(scores[t] - joint), 0.0)
         total = total + weight
         sums = sums + late[:, t : t + 1] * weight
-    @pl.when(jnp.logical_not(ahead))
-    def _():
-        span_s[...] = jnp.concatenate([joint, total], axis=0)
-        send_s[...] = sums.reshape(8, 8, 256)
-        for copy in parts:
-            copy.start()
 
     edge_s[...] = edge_rows(joint, total, sums)
 
@@ -455,6 +457,8 @@
     def _():
         for copy in downs:
             copy.start()
+
+    pl.when(has_down & jnp.logical_not(far_down))(share_own)
 
     for i in range(6, 9):
         loads[i].wait()
@@ -474,6 +478,8 @@
             head_s[...], packed_s[0:64, 0:2], packed_s[0:64, 2:4]
         )
         share(
+            far_s,
+            far_shared,
             made,
             jnp.where(packed_s[66:67] > 0.0, made_score + packed_s[64:65], FLOOR),
             packed_s[65:66],
@@ -527,11 +533,11 @@
 
     @pl.when(far_up)
     def _():
-        for copy in shared:
+        for copy in far_shared:
             copy.wait_recv()
         first_cell = lax.broadcasted_iota(jnp.int32, (16, 128), 0).astype(jnp.float32) * 16.0
         more = []
-        for tokens in [token_s[...]] + [tokens_s[k] for k in range(1, 8)]:
+        for tokens in [far_s[...]] + [fars_s[k] for k in range(1, 8)]:
             for t in range(2):
                 more.append(
                     jnp.where(
@@ -561,14 +567,12 @@
             )
         outside.append(part)
 
-    for copy in pools:
-        copy.wait_recv()
-
-    @pl.when(jnp.logical_not(far_down))
-    def _():
-        pooled_s[...] = pool_s[...].reshape(64, 256)
-
-    @pl.when(far_down)
+    @pl.when(jnp.logical_not(has_down))
+    def _():
+        scale_s[...] = jnp.ones((1, 256), jnp.float32)
+        shift_s[...] = jnp.zeros((64, 256), jnp.float32)
+
+    @pl.when(has_down)
     def _():
         for copy in shared:
             copy.wait_recv()
@@ -580,11 +584,14 @@
         all_joint = jnp.maximum(joint, jnp.max(entries, axis=0, keepdims=True))
         weight = jnp.exp(entries - all_joint)
         old = below * jnp.exp(joint - all_joint)
-        pooled_s[...] = (
-            pool_s[...].reshape(64, 256) * old + dot(rows[:, 0:64], weight, ((0,), (0,)))
-        ) / (old + jnp.sum(weight, axis=0, keepdims=True))
-
-    part0, part1, _ = split3(pooled_s[...])
+        share_of = 1.0 / (old + jnp.sum(weight, axis=0, keepdims=True))
+        scale_s[...] = old * share_of
+        shift_s[...] = dot(rows[:, 0:64], weight * share_of, ((0,), (0,)))
+
+    for copy in pools:
+        copy.wait_recv()
+    pooled = pool_s[...].reshape(64, 256) * scale_s[...] + shift_s[...]
+    part0, part1, _ = split3(pooled)
     inner = dot(
         stencil_parts,
         jnp.concatenate([part0, part0, part1], axis=0).astype(jnp.bfloat16),
@@ -619,9 +626,14 @@
     def _():
         packet.wait_send()
 
-    @pl.when(far_up | far_down)
+    @pl.when(has_down)
     def _():
         for copy in shared:
+            copy.wait_send()
+
+    @pl.when(far_up)
+    def _():
+        for copy in far_shared:
             copy.wait_send()
 
     for copy in parts + pools:
@@ -662,6 +674,9 @@
             pltpu.VMEM((72, 128), f32),
             pltpu.VMEM((8, 128), f32),
             pltpu.VMEM((8, 8, 128), f32),
+            pltpu.VMEM((8, 128), f32),
+            pltpu.VMEM((8, 8, 128), f32),
+            pltpu.VMEM((1, 256), f32),
             pltpu.VMEM((64, 256), f32),
             pltpu.VMEM((16, 64), f32),
             pltpu.VMEM((8, 8, 256), f32),
@@ -674,7 +689,7 @@
         ]
         + [dma((8,))] * 10
         + [dma((2,))]
-        + [dma((8,))] * 2
+        + [dma((8,))] * 4
         + [pltpu.SemaphoreType.REGULAR],
         compiler_params=pltpu.CompilerParams(collective_id=0, has_side_effects=True),
     )(*operands)

time: 19.6 us -> 18.8 us (0.959)
  the two profiles are of different devices: /device:TPU:1 before, /device:TPU:185 now
where the time goes in v9:
time: 18.8 us; the launch traced here: 18.6 us
  Pallas kernels  17.4 us (93%)
  between operations  0.66 us (4%)
  local copies, waits for them, and re-layouts  0.6 us (3%)
    pallas_call x1, Pallas kernels, on_device(): pl.pallas_call(kernel, out_shape=pltpu.VMEM((8, 256), f32), in_specs=[pl....  17.4 us
    unnamed x1, local copies, waits for them, and re-layouts  0.6 us

profile of v9, /device:TPU:185, one launch (start us, length us, event | category | flops | bytes accessed | tf_op | source)
XLA Modules:
  0.0 18.6 jit_solution(16927702039684852238)
XLA Ops:
  0.7 17.4 %shard_map.100 = f32[8,256]{1,0:T(8,128)S(1)} custom-call(f32[1,64,512]{2,1,0:T(8,128)} %swath_ref.1, f32[1,64,192]{2,1,0:T(8,128)} %enc_ref.1, f32[64,64]{1,0:T(8,128)} %key_ref.1, f32[64,64]{1,0:T(8,128)} %value_ref.1, f32[64,256]{1,0:T(8,128)} %query_ref.1, f32[1,512]{1,0:T(1,128)} %quality_ref.1, s32[1,512]{1,0:T(1,128)} %cell_ref.1, ...), custom_call_target="tpu_custom_call" | custom-call | tf_op jit(solution)/shard_map/pallas_call | solution.py:646
  18.0 0.6 %copy.12 = f32[8,256]{1,0:T(8,128)} copy(f32[8,256]{1,0:T(8,128)S(1)} %shard_map.100) | data formatting | bytes 16384

commit v10 on v9

--- a/solution.py
+++ b/solution.py
@@ -118,8 +118,8 @@
         pltpu.make_async_copy(source, target, in_sem.at[i])
         for i, (source, target) in enumerate(
             (
+                (cell_ref, cell_s),
                 (swath_ref.at[0], x_s),
-                (cell_ref, cell_s),
                 (query_ref, query_s),
                 (key_ref, key_s),
                 (enc_ref.at[0], enc_s),
@@ -146,7 +146,13 @@
         pl.semaphore_signal(
             barrier, inc=1, device_id=(partner(dz, dx), c), device_id_type=MESH
         )
-    for i in range(6):
+    loads[0].wait()
+    cell = cell_s[...]
+    hot_s[...] = jnp.where(
+        lax.broadcasted_iota(jnp.int32, (256, 512), 0) == cell, 1.0, 0.0
+    ).astype(jnp.bfloat16)
+
+    for i in range(1, 6):
         loads[i].wait()
     last = jnp.transpose(x_s[:, 384:512])
     row = lax.broadcasted_iota(jnp.int32, (8, 64), 0)
@@ -164,20 +170,15 @@
 
     query = query_s[...]
     bilinear = full_dot(jnp.transpose(key_s[...]) * 0.125, query)
-    cell = cell_s[...]
-    hot_s[...] = jnp.where(
-        lax.broadcasted_iota(jnp.int32, (256, 512), 0) == cell, 1.0, 0.0
-    ).astype(jnp.bfloat16)
     enc = enc_s[...]
     taps = jnp.concatenate([enc[:, 0:64], enc[:, 64:128], enc[:, 128:192]], axis=0)
     mixed = full_dot(taps, x_s[...])
-    for b in range(4):
-        index = jnp.broadcast_to(cell[:, b * 128 : (b + 1) * 128], (64, 128))
-        asked_s[:, b * 128 : (b + 1) * 128] = jnp.where(
-            index >= 128,
-            lanes(bilinear[:, 128:], index & 127),
-            lanes(bilinear[:, :128], index & 127),
-        )
+    found = dot(
+        jnp.concatenate(split3(bilinear), axis=0).astype(jnp.bfloat16),
+        hot_s[...],
+        precision=None,
+    )
+    asked_s[...] = found[0:64] + (found[64:128] + found[128:192])
     prior_s[...] = jnp.sum(query * bilinear, axis=0, keepdims=True)
 
     two, one, zero = mixed[0:64], mixed[64:128], mixed[128:192]
@@ -280,13 +281,14 @@
     peak = jnp.concatenate(halves, axis=1)
     weight = jnp.where(valid, jnp.exp(score - slot_peak), 0.0)
     weighted = jnp.concatenate(
-        [encoded * weight, jnp.broadcast_to(weight, (8, 512))], axis=0
+        [encoded * weight, jnp.broadcast_to(weight, (16, 512))], axis=0
     )
     one_hot = hot_s[...]
     turned = ((1,), (1,))
     high = weighted.astype(jnp.bfloat16)
     low = (weighted - high.astype(jnp.float32)).astype(jnp.bfloat16)
-    sums = dot(high, one_hot, turned, None) + dot(low, one_hot, turned, None)
+    sums = dot(jnp.concatenate([high, low], axis=0), one_hot, turned, None)
+    sums = sums[0:80] + sums[80:160]
     query = query_s[...]
     prior = prior_s[...]
     prior = jnp.where(s == 0, prior, FLOOR)

time: 18.8 us -> 18.8 us (level)
  no operation moved by 1% of the time
where the time goes in v10:
time: 18.8 us; the launch traced here: 18.7 us
  Pallas kernels  17.4 us (93%)
  between operations  0.66 us (4%)
  local copies, waits for them, and re-layouts  0.6 us (3%)
    pallas_call x1, Pallas kernels, on_device(): pl.pallas_call(kernel, out_shape=pltpu.VMEM((8, 256), f32), in_specs=[pl....  17.4 us
    unnamed x1, local copies, waits for them, and re-layouts  0.6 us

profile of v10, /device:TPU:185, one launch (start us, length us, event | category | flops | bytes accessed | tf_op | source)
XLA Modules:
  0.0 18.7 jit_solution(2279668274005184035)
XLA Ops:
  0.7 17.4 %shard_map.100 = f32[8,256]{1,0:T(8,128)S(1)} custom-call(f32[1,64,512]{2,1,0:T(8,128)} %swath_ref.1, f32[1,64,192]{2,1,0:T(8,128)} %enc_ref.1, f32[64,64]{1,0:T(8,128)} %key_ref.1, f32[64,64]{1,0:T(8,128)} %value_ref.1, f32[64,256]{1,0:T(8,128)} %query_ref.1, f32[1,512]{1,0:T(1,128)} %quality_ref.1, s32[1,512]{1,0:T(1,128)} %cell_ref.1, ...), custom_call_target="tpu_custom_call" | custom-call | tf_op jit(solution)/shard_map/pallas_call | solution.py:648
  18.1 0.6 %copy.12 = f32[8,256]{1,0:T(8,128)} copy(f32[8,256]{1,0:T(8,128)S(1)} %shard_map.100) | data formatting | bytes 16384

commit v11 on v10

--- a/solution.py
+++ b/solution.py
@@ -194,67 +194,9 @@
         axis=1,
     )
 
-    pl.semaphore_wait(
-        barrier, 7 + has_up.astype(jnp.int32) + has_down.astype(jnp.int32)
-    )
-    tail = pltpu.make_async_remote_copy(
-        src_ref=head_s,
-        dst_ref=tail_s,
-        send_sem=tail_sem.at[0],
-        recv_sem=tail_sem.at[1],
-        device_id=(s, up),
-        device_id_type=MESH,
-    )
-
-    @pl.when(has_up)
-    def _():
-        tail.start()
-
-    for dz, dx in OFFSETS:
-        pl.semaphore_signal(
-            ready, inc=1, device_id=(partner(dz, dx), c), device_id_type=MESH
-        )
-
-    @pl.when(jnp.logical_not(has_down))
-    def _():
-        tail_s[...] = jnp.zeros((8, 128), jnp.float32)
-        prev_s[...] = jnp.ones((8, 16, 128), jnp.float32)
-
-    @pl.when(jnp.logical_not(has_up))
-    def _():
-        next_s[...] = jnp.ones((8, 16, 128), jnp.float32)
-
     cell = cell_s[...]
     quality = quality_s[...]
     live = live_ref[0, 0]
-    packet = pltpu.make_async_remote_copy(
-        src_ref=pack_s,
-        dst_ref=packed_s,
-        send_sem=packet_sem.at[0],
-        recv_sem=packet_sem.at[1],
-        device_id=(s, down),
-        device_id_type=MESH,
-    )
-
-    @pl.when(far_down)
-    def _():
-        lane = lax.broadcasted_iota(jnp.int32, (64, 128), 1)
-        lane8 = lax.broadcasted_iota(jnp.int32, (8, 128), 1)
-        row8 = lax.broadcasted_iota(jnp.int32, (8, 128), 0)
-        pack_s[0:64] = jnp.where(
-            lane < 2, drawn[:, 0:128], pltpu.roll(asked_s[:, 0:128], 2, 1)
-        )
-        pack_s[64:72] = jnp.where(
-            row8 == 0,
-            quality[:, 0:128],
-            jnp.where(
-                row8 == 1,
-                cell[:, 0:128].astype(jnp.float32),
-                jnp.where(lane8 < live, 1.0, 0.0),
-            ),
-        )
-        packet.start()
-
     encoded = gelu(drawn)
     score = jnp.sum(encoded * asked_s[...], axis=0, keepdims=True)
     score = score + quality
@@ -298,6 +240,70 @@
     total = sums[64:65] * factor + prior_factor
     sums = sums[0:64] * factor + query * prior_factor
     peak = joint
+
+    span_s[...] = jnp.concatenate([peak, total], axis=0)
+    send_s[...] = sums.reshape(8, 8, 256)
+
+    @pl.when(far_down)
+    def _():
+        lane = lax.broadcasted_iota(jnp.int32, (64, 128), 1)
+        lane8 = lax.broadcasted_iota(jnp.int32, (8, 128), 1)
+        row8 = lax.broadcasted_iota(jnp.int32, (8, 128), 0)
+        pack_s[0:64] = jnp.where(
+            lane < 2, drawn[:, 0:128], pltpu.roll(asked_s[:, 0:128], 2, 1)
+        )
+        pack_s[64:72] = jnp.where(
+            row8 == 0,
+            quality[:, 0:128],
+            jnp.where(
+                row8 == 1,
+                cell[:, 0:128].astype(jnp.float32),
+                jnp.where(lane8 < live, 1.0, 0.0),
+            ),
+        )
+
+    pl.semaphore_wait(
+        barrier, 7 + has_up.astype(jnp.int32) + has_down.astype(jnp.int32)
+    )
+    tail = pltpu.make_async_remote_copy(
+        src_ref=head_s,
+        dst_ref=tail_s,
+        send_sem=tail_sem.at[0],
+        recv_sem=tail_sem.at[1],
+        device_id=(s, up),
+        device_id_type=MESH,
+    )
+
+    @pl.when(has_up)
+    def _():
+        tail.start()
+
+    packet = pltpu.make_async_remote_copy(
+        src_ref=pack_s,
+        dst_ref=packed_s,
+        send_sem=packet_sem.at[0],
+        recv_sem=packet_sem.at[1],
+        device_id=(s, down),
+        device_id_type=MESH,
+    )
+
+    @pl.when(far_down)
+    def _():
+        packet.start()
+
+    for dz, dx in OFFSETS:
+        pl.semaphore_signal(
+            ready, inc=1, device_id=(partner(dz, dx), c), device_id_type=MESH
+        )
+
+    @pl.when(jnp.logical_not(has_down))
+    def _():
+        tail_s[...] = jnp.zeros((8, 128), jnp.float32)
+        prev_s[...] = jnp.ones((8, 16, 128), jnp.float32)
+
+    @pl.when(jnp.logical_not(has_up))
+    def _():
+        next_s[...] = jnp.ones((8, 16, 128), jnp.float32)
 
     row = lax.broadcasted_iota(jnp.int32, (32, 256), 0)
     chosen = lax.broadcasted_iota(jnp.int32, (32, 256), 1) == (
@@ -387,8 +393,6 @@
         for copy in copies:
             copy.start()
 
-    span_s[...] = jnp.concatenate([peak, total], axis=0)
-    send_s[...] = sums.reshape(8, 8, 256)
     for copy in parts:
         copy.start()
 
@@ -512,6 +516,27 @@
         copy.start()
         pools.append(copy)
 
+    @pl.when(jnp.logical_not(has_down))
+    def _():
+        scale_s[...] = jnp.ones((1, 256), jnp.float32)
+        shift_s[...] = jnp.zeros((64, 256), jnp.float32)
+
+    @pl.when(has_down)
+    def _():
+        for copy in shared:
+            copy.wait_recv()
+        rows = jnp.concatenate(
+            [token_s[0:2]] + [tokens_s[k, 0:2] for k in range(1, 8)], axis=0
+        )
+        cells = lax.broadcasted_iota(jnp.int32, (16, 256), 1).astype(jnp.float32)
+        entries = jnp.where(cells == rows[:, 66:67], rows[:, 64:65], FLOOR)
+        all_joint = jnp.maximum(joint, jnp.max(entries, axis=0, keepdims=True))
+        weight = jnp.exp(entries - all_joint)
+        old = below * jnp.exp(joint - all_joint)
+        share_of = 1.0 / (old + jnp.sum(weight, axis=0, keepdims=True))
+        scale_s[...] = old * share_of
+        shift_s[...] = dot(rows[:, 0:64], weight * share_of, ((0,), (0,)))
+
     @pl.when(has_down)
     def _():
         for copy in ups:
@@ -568,27 +593,6 @@
                 side, lanes(outer[k * 8 : (k + 1) * 8], index), 0.0
             )
         outside.append(part)
-
-    @pl.when(jnp.logical_not(has_down))
-    def _():
-        scale_s[...] = jnp.ones((1, 256), jnp.float32)
-        shift_s[...] = jnp.zeros((64, 256), jnp.float32)
-
-    @pl.when(has_down)
-    def _():
-        for copy in shared:
-            copy.wait_recv()
-        rows = jnp.concatenate(
-            [token_s[0:2]] + [tokens_s[k, 0:2] for k in range(1, 8)], axis=0
-        )
-        cells = lax.broadcasted_iota(jnp.int32, (16, 256), 1).astype(jnp.float32)
-        entries = jnp.where(cells == rows[:, 66:67], rows[:, 64:65], FLOOR)
-        all_joint = jnp.maximum(joint, jnp.max(entries, axis=0, keepdims=True))
-        weight = jnp.exp(entries - all_joint)
-        old = below * jnp.exp(joint - all_joint)
-        share_of = 1.0 / (old + jnp.sum(weight, axis=0, keepdims=True))
-        scale_s[...] = old * share_of
-        shift_s[...] = dot(rows[:, 0:64], weight * share_of, ((0,), (0,)))
 
     for copy in pools:
         copy.wait_recv()

time: 18.8 us -> 18.5 us (0.984)
  the two profiles are of different devices: /device:TPU:185 before, /device:TPU:1 now
where the time goes in v11:
time: 18.5 us; the launch traced here: 18.4 us
  Pallas kernels  17.1 us (92%)
  between operations  0.66 us (4%)
  local copies, waits for them, and re-layouts  0.6 us (3%)
    pallas_call x1, Pallas kernels, on_device(): pl.pallas_call(kernel, out_shape=pltpu.VMEM((8, 256), f32), in_specs=[pl....  17.1 us
    unnamed x1, local copies, waits for them, and re-layouts  0.6 us

profile of v11, /device:TPU:1, one launch (start us, length us, event | category | flops | bytes accessed | tf_op | source)
XLA Modules:
  0.0 18.4 jit_solution(2404852603551944209)
XLA Ops:
  0.7 17.1 %shard_map.100 = f32[8,256]{1,0:T(8,128)S(1)} custom-call(f32[1,64,512]{2,1,0:T(8,128)} %swath_ref.1, f32[1,64,192]{2,1,0:T(8,128)} %enc_ref.1, f32[64,64]{1,0:T(8,128)} %key_ref.1, f32[64,64]{1,0:T(8,128)} %value_ref.1, f32[64,256]{1,0:T(8,128)} %query_ref.1, f32[1,512]{1,0:T(1,128)} %quality_ref.1, s32[1,512]{1,0:T(1,128)} %cell_ref.1, ...), custom_call_target="tpu_custom_call" | custom-call | tf_op jit(solution)/shard_map/pallas_call | solution.py:652
  17.8 0.6 %copy.12 = f32[8,256]{1,0:T(8,128)} copy(f32[8,256]{1,0:T(8,128)S(1)} %shard_map.100) | data formatting | bytes 16384

commit v12 on v11

--- a/solution.py
+++ b/solution.py
@@ -134,14 +134,6 @@
         load.start()
 
     barrier = pltpu.get_barrier_semaphore()
-    for target, there in ((up, has_up), (down, has_down)):
-
-        @pl.when(there)
-        def _():
-            pl.semaphore_signal(
-                barrier, inc=1, device_id=(s, target), device_id_type=MESH
-            )
-
     for dz, dx in OFFSETS:
         pl.semaphore_signal(
             barrier, inc=1, device_id=(partner(dz, dx), c), device_id_type=MESH
@@ -262,83 +254,15 @@
             ),
         )
 
-    pl.semaphore_wait(
-        barrier, 7 + has_up.astype(jnp.int32) + has_down.astype(jnp.int32)
-    )
-    tail = pltpu.make_async_remote_copy(
-        src_ref=head_s,
-        dst_ref=tail_s,
-        send_sem=tail_sem.at[0],
-        recv_sem=tail_sem.at[1],
-        device_id=(s, up),
-        device_id_type=MESH,
-    )
-
-    @pl.when(has_up)
-    def _():
-        tail.start()
-
-    packet = pltpu.make_async_remote_copy(
-        src_ref=pack_s,
-        dst_ref=packed_s,
-        send_sem=packet_sem.at[0],
-        recv_sem=packet_sem.at[1],
-        device_id=(s, down),
-        device_id_type=MESH,
-    )
-
-    @pl.when(far_down)
-    def _():
-        packet.start()
-
-    for dz, dx in OFFSETS:
-        pl.semaphore_signal(
-            ready, inc=1, device_id=(partner(dz, dx), c), device_id_type=MESH
-        )
-
-    @pl.when(jnp.logical_not(has_down))
-    def _():
-        tail_s[...] = jnp.zeros((8, 128), jnp.float32)
-        prev_s[...] = jnp.ones((8, 16, 128), jnp.float32)
-
-    @pl.when(jnp.logical_not(has_up))
-    def _():
-        next_s[...] = jnp.ones((8, 16, 128), jnp.float32)
-
-    row = lax.broadcasted_iota(jnp.int32, (32, 256), 0)
-    chosen = lax.broadcasted_iota(jnp.int32, (32, 256), 1) == (
-        (row & 15) * 16 + jnp.where(row >= 16, 15, 0)
-    )
-    chosen = jnp.where(chosen, 1.0, 0.0)
-    chosen = jnp.concatenate([chosen] * 3, axis=1).astype(jnp.bfloat16)
-
-    def edge_rows(peak, total, sums):
-        rows = jnp.concatenate(
-            [sums, peak, total, jnp.zeros((62, 256), jnp.float32)], axis=0
-        )
-        rows = jnp.concatenate(split3(rows), axis=1).astype(jnp.bfloat16)
-        return dot(chosen, rows, turned, None)
-
-    def edge_copy(source, k, cell_to, target, out, into):
-        dz, dx = (OFFSETS + ((0, 0),))[k]
-        slot = dz * 4 + dx
-        return pltpu.make_async_remote_copy(
-            src_ref=source,
-            dst_ref=target.at[slot],
-            send_sem=out.at[slot],
-            recv_sem=into.at[slot],
-            device_id=(partner(dz, dx), cell_to),
-            device_id_type=MESH,
-        )
-
-    ups = [
-        edge_copy(edge_s.at[pl.ds(16, 16)], k, up, prev_s, up_out, up_in)
-        for k in range(8)
-    ]
-    downs, far_downs = (
-        [edge_copy(source, k, down, next_s, down_out, down_in) for k in range(8)]
-        for source in (edge_s.at[pl.ds(0, 16)], early_s)
-    )
+    beside = has_up.astype(jnp.int32) + has_down.astype(jnp.int32)
+    pl.semaphore_wait(barrier, 7 + (1 - c % 2) * beside)
+    for target, there in ((up, has_up), (down, has_down)):
+
+        @pl.when(there)
+        def _():
+            pl.semaphore_signal(
+                barrier, inc=1, device_id=(s, target), device_id_type=MESH
+            )
 
     parts = []
     for dz, dx in OFFSETS:
@@ -359,6 +283,88 @@
                 )
             )
 
+    for copy in parts:
+        copy.start()
+
+    @pl.when(c % 2 == 1)
+    def _():
+        pl.semaphore_wait(barrier, beside)
+
+    tail = pltpu.make_async_remote_copy(
+        src_ref=head_s,
+        dst_ref=tail_s,
+        send_sem=tail_sem.at[0],
+        recv_sem=tail_sem.at[1],
+        device_id=(s, up),
+        device_id_type=MESH,
+    )
+
+    @pl.when(has_up)
+    def _():
+        tail.start()
+
+    packet = pltpu.make_async_remote_copy(
+        src_ref=pack_s,
+        dst_ref=packed_s,
+        send_sem=packet_sem.at[0],
+        recv_sem=packet_sem.at[1],
+        device_id=(s, down),
+        device_id_type=MESH,
+    )
+
+    @pl.when(far_down)
+    def _():
+        packet.start()
+
+    for dz, dx in OFFSETS:
+        pl.semaphore_signal(
+            ready, inc=1, device_id=(partner(dz, dx), c), device_id_type=MESH
+        )
+
+    @pl.when(jnp.logical_not(has_down))
+    def _():
+        tail_s[...] = jnp.zeros((8, 128), jnp.float32)
+        prev_s[...] = jnp.ones((8, 16, 128), jnp.float32)
+
+    @pl.when(jnp.logical_not(has_up))
+    def _():
+        next_s[...] = jnp.ones((8, 16, 128), jnp.float32)
+
+    row = lax.broadcasted_iota(jnp.int32, (32, 256), 0)
+    chosen = lax.broadcasted_iota(jnp.int32, (32, 256), 1) == (
+        (row & 15) * 16 + jnp.where(row >= 16, 15, 0)
+    )
+    chosen = jnp.where(chosen, 1.0, 0.0)
+    chosen = jnp.concatenate([chosen] * 3, axis=1).astype(jnp.bfloat16)
+
+    def edge_rows(peak, total, sums):
+        rows = jnp.concatenate(
+            [sums, peak, total, jnp.zeros((62, 256), jnp.float32)], axis=0
+        )
+        rows = jnp.concatenate(split3(rows), axis=1).astype(jnp.bfloat16)
+        return dot(chosen, rows, turned, None)
+
+    def edge_copy(source, k, cell_to, target, out, into):
+        dz, dx = (OFFSETS + ((0, 0),))[k]
+        slot = dz * 4 + dx
+        return pltpu.make_async_remote_copy(
+            src_ref=source,
+            dst_ref=target.at[slot],
+            send_sem=out.at[slot],
+            recv_sem=into.at[slot],
+            device_id=(partner(dz, dx), cell_to),
+            device_id_type=MESH,
+        )
+
+    ups = [
+        edge_copy(edge_s.at[pl.ds(16, 16)], k, up, prev_s, up_out, up_in)
+        for k in range(8)
+    ]
+    downs, far_downs = (
+        [edge_copy(source, k, down, next_s, down_out, down_in) for k in range(8)]
+        for source in (edge_s.at[pl.ds(0, 16)], early_s)
+    )
+
     shared, far_shared = (
         [
             pltpu.make_async_remote_copy(
@@ -392,9 +398,6 @@
         )
         for copy in copies:
             copy.start()
-
-    for copy in parts:
-        copy.start()
 
     @pl.when(far_down)
     def _():

time: 18.5 us -> 21.8 us (1.18)
  the two profiles are of different devices: /device:TPU:1 before, /device:TPU:257 now
where the time goes in v12:
time: 21.8 us; the launch traced here: 21.7 us
  Pallas kernels  20.4 us (94%)
  between operations  0.66 us (3%)
  local copies, waits for them, and re-layouts  0.6 us (3%)
    pallas_call x1, Pallas kernels, on_device(): pl.pallas_call(kernel, out_shape=pltpu.VMEM((8, 256), f32), in_specs=[pl....  20.4 us
    unnamed x1, local copies, waits for them, and re-layouts  0.6 us

profile of v12, /device:TPU:257, one launch (start us, length us, event | category | flops | bytes accessed | tf_op | source)
XLA Modules:
  0.0 21.7 jit_solution(16202794918959252630)
XLA Ops:
  0.7 20.4 %shard_map.100 = f32[8,256]{1,0:T(8,128)S(1)} custom-call(f32[1,64,512]{2,1,0:T(8,128)} %swath_ref.1, f32[1,64,192]{2,1,0:T(8,128)} %enc_ref.1, f32[64,64]{1,0:T(8,128)} %key_ref.1, f32[64,64]{1,0:T(8,128)} %value_ref.1, f32[64,256]{1,0:T(8,128)} %query_ref.1, f32[1,512]{1,0:T(1,128)} %quality_ref.1, s32[1,512]{1,0:T(1,128)} %cell_ref.1, ...), custom_call_target="tpu_custom_call" | custom-call | tf_op jit(solution)/shard_map/pallas_call | solution.py:655
  21.1 0.6 %copy.12 = f32[8,256]{1,0:T(8,128)} copy(f32[8,256]{1,0:T(8,128)S(1)} %shard_map.100) | data formatting | bytes 16384

commit v13 on v12

--- a/solution.py
+++ b/solution.py
@@ -130,14 +130,27 @@
             )
         )
     ]
-    for load in loads:
+    for load in loads[:6]:
         load.start()
 
     barrier = pltpu.get_barrier_semaphore()
+
+    def signal_beside(pairs):
+        for target, there in pairs:
+
+            @pl.when(there)
+            def _():
+                pl.semaphore_signal(
+                    barrier, inc=1, device_id=(s, target), device_id_type=MESH
+                )
+
+    signal_beside([(up, has_up & (c != 0)), (down, c > 1)])
     for dz, dx in OFFSETS:
         pl.semaphore_signal(
             barrier, inc=1, device_id=(partner(dz, dx), c), device_id_type=MESH
         )
+    for load in loads[6:]:
+        load.start()
     loads[0].wait()
     cell = cell_s[...]
     hot_s[...] = jnp.where(
@@ -254,16 +267,10 @@
             ),
         )
 
-    beside = has_up.astype(jnp.int32) + has_down.astype(jnp.int32)
-    pl.semaphore_wait(barrier, 7 + (1 - c % 2) * beside)
-    for target, there in ((up, has_up), (down, has_down)):
-
-        @pl.when(there)
-        def _():
-            pl.semaphore_signal(
-                barrier, inc=1, device_id=(s, target), device_id_type=MESH
-            )
-
+    first_pair = [(up, c == 0), (down, c == 1)]
+    waits = has_up.astype(jnp.int32) + has_down.astype(jnp.int32)
+    pl.semaphore_wait(barrier, 7 + jnp.where(c == 1, 1, waits))
+    signal_beside(first_pair)
     parts = []
     for dz, dx in OFFSETS:
         slot = dz * 4 + dx
@@ -286,9 +293,9 @@
     for copy in parts:
         copy.start()
 
-    @pl.when(c % 2 == 1)
-    def _():
-        pl.semaphore_wait(barrier, beside)
+    @pl.when(c == 1)
+    def _():
+        pl.semaphore_wait(barrier, 1)
 
     tail = pltpu.make_async_remote_copy(
         src_ref=head_s,

time: 21.8 us -> 19.8 us (0.908)
  the two profiles are of different devices: /device:TPU:257 before, /device:TPU:1 now
where the time goes in v13:
time: 19.8 us; the launch traced here: 19.7 us
  Pallas kernels  18.4 us (93%)
  between operations  0.66 us (3%)
  local copies, waits for them, and re-layouts  0.6 us (3%)
    pallas_call x1, Pallas kernels, on_device(): pl.pallas_call(kernel, out_shape=pltpu.VMEM((8, 256), f32), in_specs=[pl....  18.4 us
    unnamed x1, local copies, waits for them, and re-layouts  0.6 us

profile of v13, /device:TPU:1, one launch (start us, length us, event | category | flops | bytes accessed | tf_op | source)
XLA Modules:
  0.0 19.7 jit_solution(11227410448581301979)
XLA Ops:
  0.7 18.4 %shard_map.100 = f32[8,256]{1,0:T(8,128)S(1)} custom-call(f32[1,64,512]{2,1,0:T(8,128)} %swath_ref.1, f32[1,64,192]{2,1,0:T(8,128)} %enc_ref.1, f32[64,64]{1,0:T(8,128)} %key_ref.1, f32[64,64]{1,0:T(8,128)} %value_ref.1, f32[64,256]{1,0:T(8,128)} %query_ref.1, f32[1,512]{1,0:T(1,128)} %quality_ref.1, s32[1,512]{1,0:T(1,128)} %cell_ref.1, ...), custom_call_target="tpu_custom_call" | custom-call | tf_op jit(solution)/shard_map/pallas_call | solution.py:662
  19.1 0.6 %copy.12 = f32[8,256]{1,0:T(8,128)} copy(f32[8,256]{1,0:T(8,128)S(1)} %shard_map.100) | data formatting | bytes 16384

commit v14 on v13

--- a/solution.py
+++ b/solution.py
@@ -293,10 +293,6 @@
     for copy in parts:
         copy.start()
 
-    @pl.when(c == 1)
-    def _():
-        pl.semaphore_wait(barrier, 1)
-
     tail = pltpu.make_async_remote_copy(
         src_ref=head_s,
         dst_ref=tail_s,
@@ -322,6 +318,10 @@
     @pl.when(far_down)
     def _():
         packet.start()
+
+    @pl.when(c == 1)
+    def _():
+        pl.semaphore_wait(barrier, 1)
 
     for dz, dx in OFFSETS:
         pl.semaphore_signal(
@@ -460,6 +460,8 @@
 
     edge_s[...] = edge_rows(joint, total, sums)
 
+    pl.when(c == 1)(share_own)
+
     @pl.when(jnp.logical_not(far_down))
     def _():
         pl.semaphore_wait(ready, 7)
@@ -474,7 +476,7 @@
         for copy in downs:
             copy.start()
 
-    pl.when(has_down & jnp.logical_not(far_down))(share_own)
+    pl.when((c > 1) & jnp.logical_not(far_down))(share_own)
 
     for i in range(6, 9):
         loads[i].wait()

time: 19.8 us -> 18.7 us (0.944)
  Pallas kernels: 18.4 us -> 17.3 us
    pallas_call x1, Pallas kernels: 18.4 us -> 17.3 us  [on_device(): pl.pallas_call(kernel, out_shape=pltpu.VMEM((8, 256), f32), in_specs=[pl....]
where the time goes in v14:
time: 18.7 us; the launch traced here: 18.6 us
  Pallas kernels  17.3 us (93%)
  between operations  0.66 us (4%)
  local copies, waits for them, and re-layouts  0.6 us (3%)
    pallas_call x1, Pallas kernels, on_device(): pl.pallas_call(kernel, out_shape=pltpu.VMEM((8, 256), f32), in_specs=[pl....  17.3 us
    unnamed x1, local copies, waits for them, and re-layouts  0.6 us

profile of v14, /device:TPU:1, one launch (start us, length us, event | category | flops | bytes accessed | tf_op | source)
XLA Modules:
  0.0 18.6 jit_solution(9138421497131953353)
XLA Ops:
  0.7 17.3 %shard_map.100 = f32[8,256]{1,0:T(8,128)S(1)} custom-call(f32[1,64,512]{2,1,0:T(8,128)} %swath_ref.1, f32[1,64,192]{2,1,0:T(8,128)} %enc_ref.1, f32[64,64]{1,0:T(8,128)} %key_ref.1, f32[64,64]{1,0:T(8,128)} %value_ref.1, f32[64,256]{1,0:T(8,128)} %query_ref.1, f32[1,512]{1,0:T(1,128)} %quality_ref.1, s32[1,512]{1,0:T(1,128)} %cell_ref.1, ...), custom_call_target="tpu_custom_call" | custom-call | tf_op jit(solution)/shard_map/pallas_call | solution.py:664
  18.0 0.6 %copy.12 = f32[8,256]{1,0:T(8,128)} copy(f32[8,256]{1,0:T(8,128)S(1)} %shard_map.100) | data formatting | bytes 16384

commit v15 on v13

--- a/solution.py
+++ b/solution.py
@@ -135,16 +135,14 @@
 
     barrier = pltpu.get_barrier_semaphore()
 
-    def signal_beside(pairs):
-        for target, there in pairs:
-
-            @pl.when(there)
-            def _():
-                pl.semaphore_signal(
-                    barrier, inc=1, device_id=(s, target), device_id_type=MESH
-                )
-
-    signal_beside([(up, has_up & (c != 0)), (down, c > 1)])
+    for target, there in ((up, has_up), (down, has_down)):
+
+        @pl.when(there)
+        def _():
+            pl.semaphore_signal(
+                barrier, inc=1, device_id=(s, target), device_id_type=MESH
+            )
+
     for dz, dx in OFFSETS:
         pl.semaphore_signal(
             barrier, inc=1, device_id=(partner(dz, dx), c), device_id_type=MESH
@@ -267,10 +265,9 @@
             ),
         )
 
-    first_pair = [(up, c == 0), (down, c == 1)]
-    waits = has_up.astype(jnp.int32) + has_down.astype(jnp.int32)
-    pl.semaphore_wait(barrier, 7 + jnp.where(c == 1, 1, waits))
-    signal_beside(first_pair)
+    pl.semaphore_wait(
+        barrier, 7 + has_up.astype(jnp.int32) + has_down.astype(jnp.int32)
+    )
     parts = []
     for dz, dx in OFFSETS:
         slot = dz * 4 + dx
@@ -292,10 +289,6 @@
 
     for copy in parts:
         copy.start()
-
-    @pl.when(c == 1)
-    def _():
-        pl.semaphore_wait(barrier, 1)
 
     tail = pltpu.make_async_remote_copy(
         src_ref=head_s,

time: 19.8 us -> 18.6 us (0.939)
  the two profiles are of different devices: /device:TPU:1 before, /device:TPU:185 now
where the time goes in v15:
time: 18.6 us; the launch traced here: 18.4 us
  Pallas kernels  17.2 us (92%)
  between operations  0.66 us (4%)
  local copies, waits for them, and re-layouts  0.6 us (3%)
    pallas_call x1, Pallas kernels, on_device(): pl.pallas_call(kernel, out_shape=pltpu.VMEM((8, 256), f32), in_specs=[pl....  17.2 us
    unnamed x1, local copies, waits for them, and re-layouts  0.6 us

profile of v15, /device:TPU:185, one launch (start us, length us, event | category | flops | bytes accessed | tf_op | source)
XLA Modules:
  0.0 18.4 jit_solution(12275215791056256976)
XLA Ops:
  0.7 17.2 %shard_map.100 = f32[8,256]{1,0:T(8,128)S(1)} custom-call(f32[1,64,512]{2,1,0:T(8,128)} %swath_ref.1, f32[1,64,192]{2,1,0:T(8,128)} %enc_ref.1, f32[64,64]{1,0:T(8,128)} %key_ref.1, f32[64,64]{1,0:T(8,128)} %value_ref.1, f32[64,256]{1,0:T(8,128)} %query_ref.1, f32[1,512]{1,0:T(1,128)} %quality_ref.1, s32[1,512]{1,0:T(1,128)} %cell_ref.1, ...), custom_call_target="tpu_custom_call" | custom-call | tf_op jit(solution)/shard_map/pallas_call | solution.py:655
  17.8 0.6 %copy.12 = f32[8,256]{1,0:T(8,128)} copy(f32[8,256]{1,0:T(8,128)S(1)} %shard_map.100) | data formatting | bytes 16384

commit v16 on v15

--- a/solution.py
+++ b/solution.py
@@ -106,13 +106,16 @@
 ):
     s = lax.axis_index("sensor")
     c = lax.axis_index("cell")
-    z, x = s // 4, s % 4
+    z, x = lax.div(s, 4), lax.rem(s, 4)
     up, down = c + 1, c - 1
     has_up, has_down = c < 63, c > 0
     far_up, far_down = has_up & (c % 16 == 15), has_down & (c % 16 == 0)
 
+    rows = (z * 4, (1 - z) * 4)
+    columns = [x] + [lax.rem(x + k, 4) for k in range(1, 4)]
+
     def partner(dz, dx):
-        return ((z + dz) % 2) * 4 + (x + dx) % 4
+        return rows[dz] + columns[dx]
 
     loads = [
         pltpu.make_async_copy(source, target, in_sem.at[i])

time: 18.6 us -> 18.6 us (level)
  no operation moved by 1% of the time
where the time goes in v16:
time: 18.6 us; the launch traced here: 18.4 us
  Pallas kernels  17.2 us (92%)
  between operations  0.66 us (4%)
  local copies, waits for them, and re-layouts  0.6 us (3%)
    pallas_call x1, Pallas kernels, on_device(): pl.pallas_call(kernel, out_shape=pltpu.VMEM((8, 256), f32), in_specs=[pl....  17.2 us
    unnamed x1, local copies, waits for them, and re-layouts  0.6 us

profile of v16, /device:TPU:185, one launch (start us, length us, event | category | flops | bytes accessed | tf_op | source)
XLA Modules:
  0.0 18.4 jit_solution(13237186525827407070)
XLA Ops:
  0.7 17.2 %shard_map.100 = f32[8,256]{1,0:T(8,128)S(1)} custom-call(f32[1,64,512]{2,1,0:T(8,128)} %swath_ref.1, f32[1,64,192]{2,1,0:T(8,128)} %enc_ref.1, f32[64,64]{1,0:T(8,128)} %key_ref.1, f32[64,64]{1,0:T(8,128)} %value_ref.1, f32[64,256]{1,0:T(8,128)} %query_ref.1, f32[1,512]{1,0:T(1,128)} %quality_ref.1, s32[1,512]{1,0:T(1,128)} %cell_ref.1, ...), custom_call_target="tpu_custom_call" | custom-call | tf_op jit(solution)/shard_map/pallas_call | solution.py:658
  17.8 0.6 %copy.12 = f32[8,256]{1,0:T(8,128)} copy(f32[8,256]{1,0:T(8,128)S(1)} %shard_map.100) | data formatting | bytes 16384
